TPU v7x, 512 devices: a whole 4x4x16 slice. The times are simulated.
512 devices in a mesh: rows: 64 (over z, x), samp: 8 (over y, core).
Axes of the slice: x: 4, y: 4, z: 16, core: 2. Of those that a mesh axis runs over, the one named last changes fastest.
Arguments:
- sketch: float32 [256, 786432], P('samp', 'rows'), may hold values from -6 to 6
- probes: float32 [256, 786432], P('samp', 'rows'), may hold values from -6 to 6
- test_leaf: float32 [64, 256], replicated, may hold values from -0.375 to 0.375
- test_parent: float32 [64, 256], replicated, may hold values from -0.375 to 0.375
- leaf_far: int32 [3072, 8], P(('rows', 'samp')), may hold values from 0 to 3071, as said below
- leaf_count: int32 [3072], P(('rows', 'samp')), may hold values from 1 to 8
- parent_far: int32 [1536, 8], P(('rows', 'samp')), may hold values from 0 to 1535, as said below
- parent_count: int32 [1536], P(('rows', 'samp')), may hold values from 1 to 8
Outputs:
- leaf_basis: float32 [64, 786432], P(None, ('rows', 'samp'))
- leaf_coupling: float32 [3072, 8, 4096], P(('rows', 'samp'))
- transfer: float32 [1536, 64, 128], P(('rows', 'samp'))
- parent_coupling: float32 [1536, 8, 4096], P(('rows', 'samp'))
Inputs may be any that keep to these rules, and one draw needn't show every extreme that they name: leaf_far[i, k] = j satisfies 2 <= |i - j| <= 6. `parent_far`: with b(p) = p // 3, a partner q of p has b(q) - b(p) a nonzero multiple of 8, at most 4 * 8 in magnitude.
All inputs are finite; a program needn't handle non-finite values.
Results may differ from a plain program's by a relative error of at most 0.0041.
Values may be sent and summed in bfloat16 or wider, within the bound.
No kernel may reach another device: no remote copies, remote signals or barrier semaphores. Data moves between devices by JAX's collectives and lax.ppermute only.
A program may use at most 64 MiB of HBM per device.

v0:
```python
import functools
import jax
import jax.numpy as jnp
from jax import lax
from jax.experimental import pallas as pl
from jax.experimental.pallas import tpu as pltpu
from jax.sharding import PartitionSpec as P

f32 = jnp.float32
bf16 = jnp.bfloat16

LEAF = 256
RANK = 64
REACH = 4
SCALE = 8192.0


def split(x):
    high = x.astype(bf16)
    low = (x - high.astype(f32)).astype(bf16)
    return high, low


def product(a, b, contract):
    dims = ((contract[0],), (contract[1],)), ((), ())
    dot = functools.partial(lax.dot_general, dimension_numbers=dims, preferred_element_type=f32)
    return dot(a[0], b[0]) + (dot(a[1], b[0]) + dot(a[0], b[1]))


def inverse_factors(packs):
    tiles = RANK // 8
    lane = lax.broadcasted_iota(jnp.int32, (8, 128), 1)
    sub = lax.broadcasted_iota(jnp.int32, (8, 128), 0)
    column = lane % RANK
    half = lane - column

    def row(x, k):
        return jnp.broadcast_to(x[k : k + 1, :], (8, 128))

    state = [[p[8 * t : 8 * t + 8, :] for t in range(tiles)] for p in packs]
    for block in range(tiles):
        start = 8 * block
        cols = [
            [
                [jnp.take_along_axis(s[t], half + (start + k), axis=1) for t in range(block, tiles)]
                for k in range(8)
            ]
            for s in state
        ]
        inside = (column >= start) & (column < start + 8)
        unit = jnp.where(column == start + sub, 1.0, 0.0).astype(f32)
        for s, c in zip(state, cols):
            head = jnp.where(inside, unit, s[block])
            rest = [jnp.where(inside, 0.0, s[t]) for t in range(block + 1, tiles)]
            pivots = jnp.ones((8, 128), f32)
            for k in range(8):
                pivot = row(c[k][0], k)
                pivots = jnp.where(sub == k, pivot, pivots)
                inv = 1.0 / pivot
                mult = [x * inv for x in c[k]]
                mult[0] = jnp.where(sub > k, mult[0], 0.0)
                for k2 in range(k + 1, 8):
                    factor = row(c[k][0], k2)
                    c[k2] = [x - m * factor for x, m in zip(c[k2], mult)]
                lead = row(head, k)
                head = head - mult[0] * lead
                rest = [x - m * lead for x, m in zip(rest, mult[1:])]
            head = head * lax.rsqrt(pivots)
            s[block] = jnp.where(column <= start + sub, head, 0.0)
            s[block + 1 :] = rest
    return [jnp.concatenate(s, axis=0) for s in state]


def inverses(grams):
    padded = list(grams) + ([grams[-1]] if len(grams) % 2 else [])
    packs = [jnp.concatenate(padded[i : i + 2], axis=1) for i in range(0, len(padded), 2)]
    done = inverse_factors(packs)
    out = []
    for p in done:
        out += [p[:, :RANK], p[:, RANK:]]
    return out[: len(grams)]


def keep(halves, i, value):
    for h, half in enumerate(halves):
        half[RANK * i : RANK * i + RANK, :] = value[:, 128 * h : 128 * h + 128]


def deinterleave(halves, i, out_ref):
    for h, half in enumerate(halves):
        for odd in range(2):
            rows = half[pl.ds(RANK * i + odd, RANK // 2, stride=2), :]
            start = RANK * i + RANK // 2 * odd
            out_ref[start : start + RANK // 2, 128 * h : 128 * h + 128] = rows.astype(bf16)


def compress(y_ref, test_ref, ptest_ref, basis_ref, w_ref, transfer_ref, a_ref, *halves):
    owned = y_ref.shape[1] // LEAF
    parents = owned // 2
    test = split(test_ref[...])
    ys, ks, grams = [], [], []
    for i in range(owned):
        y = split(y_ref[:, LEAF * i : LEAF * i + LEAF])
        ys.append(y)
        k = split(product(test, y, (1, 0)))
        ks.append(k)
        grams.append(product(k, k, (1, 1)))
    linvs = inverses(grams)
    ptest = split(ptest_ref[...])
    for i in range(owned):
        q = product(split(linvs[i]), ks[i], (1, 0))
        basis_ref[:, LEAF * i : LEAF * i + LEAF] = q
        keep(halves, i, product(split(q), ys[i], (1, 1)))
    blocks, stacks, grams = [], [], []
    for p in range(parents):
        stack = [h[2 * RANK * p : 2 * RANK * (p + 1), :] for h in halves]
        stack = split(jnp.concatenate(stack, axis=1))
        stacks.append(stack)
        c = split(product(ptest, stack, (1, 1)))
        blocks.append(c)
        grams.append(product(c, c, (1, 1)))
    for i in range(owned):
        deinterleave(halves, i, w_ref)
    finvs = inverses(grams)
    for p in range(parents):
        x = product(split(finvs[p]), blocks[p], (1, 0))
        transfer_ref[p] = x
        keep(halves, p, product(split(x), stacks[p], (1, 0)))
        deinterleave(halves, p, a_ref)


def project(o_ref, basis_ref, transfer_ref, v_ref, b_ref):
    owned = o_ref.shape[1] // LEAF
    for p in range(owned // 2):
        pair = []
        for i in (2 * p, 2 * p + 1):
            q = split(basis_ref[:, LEAF * i : LEAF * i + LEAF])
            v = product(q, split(o_ref[:, LEAF * i : LEAF * i + LEAF]), (1, 1))
            v_ref[RANK * i : RANK * i + RANK, :] = v.astype(bf16)
            pair.append(v)
        stack = split(jnp.concatenate(pair, axis=0))
        b_ref[RANK * p : RANK * p + RANK, :] = product(split(transfer_ref[p]), stack, (1, 0)).astype(bf16)


def couple(far_ref, count_ref, left_ref, *refs):
    pieces, out_ref, table = refs[:-2], refs[-2], refs[-1]
    rows = left_ref.shape[0] // RANK
    slots = far_ref.shape[1]
    at = 0
    for piece in pieces:
        size = piece.shape[0] // RANK
        for j in range(size):
            table[at + j] = piece[RANK * j : RANK * j + RANK, :]
        at += size
    lane = lax.broadcasted_iota(jnp.int32, (RANK // 2, 128), 1)
    low = lane < RANK
    samples = left_ref.shape[1]
    dims = (((1,), (1,)), ((), ()))
    for i in range(rows):
        left = left_ref[RANK * i : RANK * i + RANK, :]
        for k in range(0, slots, 2):
            right = jnp.concatenate([table[far_ref[i, k + e]] for e in range(2)], axis=0)
            x = lax.dot_general(left, right, dims, preferred_element_type=f32)
            even, odd = x[: RANK // 2], x[RANK // 2 :]
            first = jnp.where(low, even, pltpu.roll(odd, RANK, 1))
            second = jnp.where(low, pltpu.roll(even, RANK, 1), odd)
            for e, value in enumerate((first, second)):
                scale = jnp.where(k + e < count_ref[i], 1.0 / samples, 0.0).astype(f32)
                out_ref[pl.ds(i * 4 * RANK + k + e, RANK // 2, stride=8), :] = value * scale


vmem = pl.BlockSpec(memory_space=pltpu.VMEM)
smem = pl.BlockSpec(memory_space=pltpu.SMEM)


def run_compress(y, test, ptest):
    owned = y.shape[1] // LEAF
    samples = y.shape[0]
    return pl.pallas_call(
        compress,
        out_shape=(
            jax.ShapeDtypeStruct((RANK, y.shape[1]), f32),
            jax.ShapeDtypeStruct((owned * RANK, samples), bf16),
            jax.ShapeDtypeStruct((owned // 2, RANK, 2 * RANK), f32),
            jax.ShapeDtypeStruct((owned // 2 * RANK, samples), bf16),
        ),
        in_specs=[vmem] * 3,
        out_specs=(vmem,) * 4,
        scratch_shapes=[pltpu.VMEM((owned * RANK, 128), f32)] * (samples // 128),
        name="compress",
    )(y, test, ptest)


def run_project(o, basis, transfer):
    owned = o.shape[1] // LEAF
    samples = o.shape[0]
    return pl.pallas_call(
        project,
        out_shape=(
            jax.ShapeDtypeStruct((owned * RANK, samples), bf16),
            jax.ShapeDtypeStruct((owned // 2 * RANK, samples), bf16),
        ),
        in_specs=[vmem] * 3,
        out_specs=(vmem,) * 2,
        name="project",
    )(o, basis, transfer)


def run_couple(far, count, left, pieces, name):
    rows, slots = far.shape
    total = sum(p.shape[0] for p in pieces) // RANK
    out = pl.pallas_call(
        couple,
        out_shape=jax.ShapeDtypeStruct((rows * 4 * RANK, 128), f32),
        in_specs=[smem, smem, vmem] + [vmem] * len(pieces),
        out_specs=vmem,
        scratch_shapes=[pltpu.VMEM((total, RANK, left.shape[1]), bf16)],
        name=name,
    )(far, count, left, *pieces)
    out = out.reshape(rows, RANK // 2, slots, 128)
    return out.transpose(0, 2, 1, 3).reshape(rows, slots, RANK * RANK)


def gathered(array):
    devices = lax.axis_size("samp")
    rows, columns = array.shape
    sent = (array * SCALE).astype(jnp.float16).reshape(rows, devices, columns // devices).transpose(1, 0, 2)
    got = lax.all_to_all(sent, "samp", split_axis=0, concat_axis=0, tiled=True)
    return got.astype(f32).reshape(rows * devices, columns // devices) * (1.0 / SCALE)


def shifted(array, axis, by):
    devices = lax.axis_size(axis)
    pairs = [(i, (i - by) % devices) for i in range(devices)]
    return lax.ppermute(array, axis, pairs)


def body(sketch, probes, test_leaf, test_parent, leaf_far, leaf_count, parent_far, parent_count):
    owned = leaf_far.shape[0]
    per_device = parent_far.shape[0]
    y = gathered(sketch)
    o = gathered(probes)
    basis, w, transfer, a = run_compress(y, test_leaf, test_parent)
    v, b = run_project(o, basis, transfer)
    before, after = shifted(b, "rows", -1), shifted(b, "rows", 1)
    near = jnp.concatenate([before, b, after], axis=0)
    v_before, v_after = shifted(v, ("rows", "samp"), -1), shifted(v, ("rows", "samp"), 1)
    far_before, far_after = shifted(near, "rows", -3), shifted(near, "rows", 3)
    first_leaf = lax.axis_index(("rows", "samp")) * owned
    leaf_at = jnp.clip(leaf_far - first_leaf + owned, 0, 3 * owned - 1)
    leaf_coupling = run_couple(leaf_at, leaf_count, w, [v_before, v, v_after], "leaf")
    row = parent_far // (per_device * lax.axis_size("samp"))
    step = row - lax.axis_index("rows") + REACH
    parent_at = jnp.clip(step * per_device + parent_far % per_device, 0, (2 * REACH + 1) * per_device - 1)
    parent_coupling = run_couple(parent_at, parent_count, a, [far_before, near, far_after], "parent")
    return (basis, leaf_coupling, transfer, parent_coupling)


def solution(mesh):
    return jax.shard_map(
        body,
        mesh=mesh,
        in_specs=(
            P("samp", "rows"),
            P("samp", "rows"),
            P(),
            P(),
            P(("rows", "samp"), None),
            P(("rows", "samp")),
            P(("rows", "samp"), None),
            P(("rows", "samp")),
        ),
        out_specs=(
            P(None, ("rows", "samp")),
            P(("rows", "samp"), None, None),
            P(("rows", "samp"), None, None),
            P(("rows", "samp"), None, None),
        ),
        check_vma=False,
    )
```

profile of v0, /device:TPU:27, one launch (start us, length us, event | category | flops | bytes accessed | tf_op | source)
XLA Modules:
  0.0 88.4 jit_solution(4125913904342500216)
XLA Ops:
  0.6 1.5 %multiply_convert_fusion.1 = f16[32,12288]{1,0:T(8,128)(2,1)S(1)} fusion(f32[32,12288]{1,0:T(8,128)} %param.8), kind=kLoop, calls=%fused_computation.3 | loop fusion | flops 786432 | bytes 2359296 | tf_op jit(solution)/shard_map/convert_element_type | solution.py:227
  2.2 0.0 copy-start
  2.2 1.0 %copy.19 = f16[4,8,8,1536]{3,2,0,1:T(8,128)(2,1)} copy(f16[4,8,8,1536]{3,2,1,0:T(8,128)(2,1)S(1)} %bitcast.28) | data formatting | bytes 1572864 | tf_op jit(solution)/shard_map/reshape | solution.py:227
  3.2 5.0 %all-to-all-start = ((f16[8,32,1536]{2,1,0:T(8,128)(2,1)}), f16[8,32,1536]{2,1,0:T(8,128)(2,1)S(1)}, u32[]{:S(2)}, u32[]{:S(2)}) async-start(f16[8,32,1536]{2,1,0:T(8,128)(2,1)} %bitcast.25), calls=%async_computation | async-start | bytes 1572864 | tf_op jit(solution)/shard_map/all_to_all | solution.py:228
  8.2 0.0 copy-done
  8.2 0.1 multiply_convert_fusion
  8.3 1.0 %copy.18 = f16[4,8,8,1536]{3,2,0,1:T(8,128)(2,1)} copy(f16[4,8,8,1536]{3,2,1,0:T(8,128)(2,1)S(1)} %bitcast.29) | data formatting | bytes 1572864 | tf_op jit(solution)/shard_map/reshape | solution.py:227
  9.3 9.3 %all-to-all-done = f16[8,32,1536]{2,1,0:T(8,128)(2,1)S(1)} async-done(((f16[8,32,1536]{2,1,0:T(8,128)(2,1)}), f16[8,32,1536]{2,1,0:T(8,128)(2,1)S(1)}, u32[]{:S(2)}, u32[]{:S(2)}) %all-to-all-start) | async-done | bytes 786464 | tf_op jit(solution)/shard_map/all_to_all | solution.py:228
  18.6 6.1 %all-to-all-start.1 = ((f16[8,32,1536]{2,1,0:T(8,128)(2,1)}), f16[8,32,1536]{2,1,0:T(8,128)(2,1)S(1)}, u32[]{:S(2)}, u32[]{:S(2)}) async-start(f16[8,32,1536]{2,1,0:T(8,128)(2,1)} %bitcast.23), calls=%async_computation.1 | async-start | bytes 1572864 | tf_op jit(solution)/shard_map/all_to_all | solution.py:228
  24.8 1.4 %convert_multiply_fusion.1 = f32[8,32,1536]{2,1,0:T(8,128)} fusion(f16[8,32,1536]{2,1,0:T(8,128)(2,1)S(1)} %all-to-all-done), kind=kLoop, calls=%fused_computation.2 | loop fusion | flops 786432 | bytes 2359296 | tf_op jit(solution)/shard_map/mul | solution.py:229
  26.2 10.5 %compress.1 = (f32[64,1536]{1,0:T(8,128)}, bf16[384,256]{1,0:T(8,128)(2,1)}, f32[3,64,128]{2,1,0:T(8,128)}, bf16[192,256]{1,0:T(8,128)(2,1)}) custom-call(f32[256,1536]{1,0:T(8,128)} %bitcast.26, f32[64,256]{1,0:T(8,128)} %test_ref.1, f32[64,256]{1,0:T(8,128)} %ptest_ref.1), custom_call_target="tpu_custom_call" | custom-call | tf_op jit(solution)/shard_map/compress/pallas_call | solution.py:179
  36.7 0.0 all-to-all-done.1
  36.7 1.4 %convert_multiply_fusion = f32[8,32,1536]{2,1,0:T(8,128)} fusion(f16[8,32,1536]{2,1,0:T(8,128)(2,1)S(1)} %all-to-all-done.1), kind=kLoop, calls=%fused_computation | loop fusion | flops 786432 | bytes 2359296 | tf_op jit(solution)/shard_map/mul | solution.py:229
  38.1 0.0 copy-start.6
  38.1 0.0 copy-start.7
  38.1 3.5 %project.1 = (bf16[384,256]{1,0:T(8,128)(2,1)}, bf16[192,256]{1,0:T(8,128)(2,1)}) custom-call(f32[256,1536]{1,0:T(8,128)} %bitcast.27, f32[64,1536]{1,0:T(8,128)} %get-tuple-element.6.basis_ref, f32[3,64,128]{2,1,0:T(8,128)} %get-tuple-element.8.transfer_ref), custom_call_target="tpu_custom_call" | custom-call | tf_op jit(solution)/shard_map/project/pallas_call | solution.py:197
  41.6 3.1 %collective-permute-start.2 = (bf16[192,256]{1,0:T(8,128)(2,1)}, bf16[192,256]{1,0:T(8,128)(2,1)S(1)}, u32[]{:S(2)}, u32[]{:S(2)}) collective-permute-start(bf16[192,256]{1,0:T(8,128)(2,1)} %get-tuple-element.15), channel_id=1, source_target_pairs={{0,8},{8,16},{16,24},{24,32},{32,40},{40,48},{48,56},{56,64},{64,7... | collective-permute-start | bytes 294920 | tf_op jit(solution)/shard_map/ppermute | solution.py:235
  44.8 5.3 %collective-permute-start.3 = (bf16[192,256]{1,0:T(8,128)(2,1)}, bf16[192,256]{1,0:T(8,128)(2,1)S(1)}, u32[]{:S(2)}, u32[]{:S(2)}) collective-permute-start(bf16[192,256]{1,0:T(8,128)(2,1)} %get-tuple-element.15), channel_id=1, source_target_pairs={{0,504},{8,0},{16,8},{24,16},{32,24},{40,32},{48,40},{56,48},{64,5... | collective-permute-start | bytes 294920 | tf_op jit(solution)/shard_map/ppermute | solution.py:235
  50.1 1.0 %collective-permute-done.2 = bf16[192,256]{1,0:T(8,128)(2,1)S(1)} collective-permute-done((bf16[192,256]{1,0:T(8,128)(2,1)}, bf16[192,256]{1,0:T(8,128)(2,1)S(1)}, u32[]{:S(2)}, u32[]{:S(2)}) %collective-permute-start.2) | collective-permute-done | bytes 98336 | tf_op jit(solution)/shard_map/ppermute | solution.py:235
  51.1 0.9 %constant_dynamic-update-slice_fusion.1 = bf16[576,256]{1,0:T(8,128)(2,1)S(1)} fusion(bf16[576,256]{1,0:T(8,128)(2,1)S(1)} %constant_dynamic-update-slice_fusion.2, bf16[192,256]{1,0:T(8,128)(2,1)} %get-tuple-element.15), kind=kLoop, calls=%fused_computation.7 | loop fusion | bytes 196608
  52.0 0.1 collective-permute-done.3
  52.2 0.0 copy-start.1
  52.2 2.3 %collective-permute-start.4 = (bf16[576,256]{1,0:T(8,128)(2,1)S(1)}, bf16[576,256]{1,0:T(8,128)(2,1)S(1)}, u32[]{:S(2)}, u32[]{:S(2)}) collective-permute-start(bf16[576,256]{1,0:T(8,128)(2,1)S(1)} %constant_dynamic-update-slice_fusion.refs_1_), channel_id=1, source_target_pairs={{0,24},{8,32},{16,40},{24,48},{32,56},{40,64},{48,72},{56,80},{64,... | collective-permute-start | bytes 884744 | tf_op jit(solution)/shard_map/ppermute | solution.py:235
  54.5 9.5 %collective-permute-start.5 = (bf16[576,256]{1,0:T(8,128)(2,1)S(1)}, bf16[576,256]{1,0:T(8,128)(2,1)S(1)}, u32[]{:S(2)}, u32[]{:S(2)}) collective-permute-start(bf16[576,256]{1,0:T(8,128)(2,1)S(1)} %constant_dynamic-update-slice_fusion.refs_1_), channel_id=1, source_target_pairs={{0,488},{8,496},{16,504},{24,0},{32,8},{40,16},{48,24},{56,32},{64... | collective-permute-start | bytes 884744 | tf_op jit(solution)/shard_map/ppermute | solution.py:235
  64.1 0.0 copy-done.6
  64.1 0.6 add_clamp_fusion.far_ref
  64.7 7.5 %collective-permute-start = (bf16[384,256]{1,0:T(8,128)(2,1)}, bf16[384,256]{1,0:T(8,128)(2,1)S(1)}, u32[]{:S(2)}, u32[]{:S(2)}) collective-permute-start(bf16[384,256]{1,0:T(8,128)(2,1)} %get-tuple-element.13.refs_1_), channel_id=1, source_target_pairs={{0,1},{1,2},{2,3},{3,4},{4,5},{5,6},{6,7},{7,8},{8,9},{9,10},{10,1... | collective-permute-start | bytes 589832 | tf_op jit(solution)/shard_map/ppermute | solution.py:235
  72.2 1.9 %collective-permute-start.1 = (bf16[384,256]{1,0:T(8,128)(2,1)}, bf16[384,256]{1,0:T(8,128)(2,1)S(1)}, u32[]{:S(2)}, u32[]{:S(2)}) collective-permute-start(bf16[384,256]{1,0:T(8,128)(2,1)} %get-tuple-element.13.refs_1_), channel_id=1, source_target_pairs={{0,511},{1,0},{2,1},{3,2},{4,3},{5,4},{6,5},{7,6},{8,7},{9,8},{10,... | collective-permute-start | bytes 589832 | tf_op jit(solution)/shard_map/ppermute | solution.py:235
  74.1 0.0 copy-done.7
  74.2 0.6 fusion.1.far_ref
  74.8 0.4 collective-permute-done.refs_0_
  75.1 0.0 copy-start.4
  75.1 6.4 %collective-permute-done.1.refs_2_ = bf16[384,256]{1,0:T(8,128)(2,1)S(1)} collective-permute-done((bf16[384,256]{1,0:T(8,128)(2,1)}, bf16[384,256]{1,0:T(8,128)(2,1)S(1)}, u32[]{:S(2)}, u32[]{:S(2)}) %collective-permute-start.1) | collective-permute-done | bytes 196640 | tf_op jit(solution)/shard_map/ppermute | solution.py:235
  81.5 0.0 copy-start.5
  81.5 0.0 copy-done.4
  81.5 0.7 copy-done.5
  82.2 2.9 %leaf.1 = f32[1536,128]{1,0:T(8,128)} custom-call(s32[6,8]{1,0:T(8,128)} %add_clamp_fusion.far_ref, s32[6]{0:T(128)} %count_ref.2, bf16[384,256]{1,0:T(8,128)(2,1)} %get-tuple-element.11.left_ref, bf16[384,256]{1,0:T(8,128)(2,1)} %copy-done.4, bf16[384,256]{1,0:T(8,128)(2,1)} %get-tuple-element.13.refs_1_, bf16[384,256]{1,0:T(8,128)(2,1)} %copy-done.5), custom_call_target="tpu_custom_call" | custom-call | tf_op jit(solution)/shard_map/leaf/pallas_call | solution.py:212
  85.1 0.0 collective-permute-done.4.refs_0_
  85.1 0.0 copy-start.2
  85.1 0.0 collective-permute-done.5.refs_2_
  85.1 0.0 copy-start.3
  85.1 0.0 copy-done.1
  85.1 0.7 copy-done.2
  85.8 0.1 copy-done.3
  85.9 2.5 %parent.1 = f32[768,128]{1,0:T(8,128)} custom-call(s32[3,8]{1,0:T(4,128)} %fusion.1.far_ref, s32[3]{0:T(128)} %count_ref.3, bf16[192,256]{1,0:T(8,128)(2,1)} %get-tuple-element.14.left_ref, bf16[576,256]{1,0:T(8,128)(2,1)} %copy-done.2, bf16[576,256]{1,0:T(8,128)(2,1)} %copy-done.1, bf16[576,256]{1,0:T(8,128)(2,1)} %copy-done.3), custom_call_target="tpu_custom_call" | custom-call | tf_op jit(solution)/shard_map/parent/pallas_call | solution.py:212
  (2 shorter events, 0.0 us)
Async XLA Ops:
  2.2 6.0 %copy-start = (f32[32,12288]{1,0:T(8,128)S(1)}, f32[32,12288]{1,0:T(8,128)}, u32[]{:S(2)}) copy-start(f32[32,12288]{1,0:T(8,128)} %param.9) | copy-start | bytes 4718596
  3.2 15.5 %all-to-all-start = ((f16[8,32,1536]{2,1,0:T(8,128)(2,1)}), f16[8,32,1536]{2,1,0:T(8,128)(2,1)S(1)}, u32[]{:S(2)}, u32[]{:S(2)}) async-start(f16[8,32,1536]{2,1,0:T(8,128)(2,1)} %bitcast.25), calls=%async_computation | async-start | bytes 1572864 | tf_op jit(solution)/shard_map/all_to_all | solution.py:228
  18.6 18.1 %all-to-all-start.1 = ((f16[8,32,1536]{2,1,0:T(8,128)(2,1)}), f16[8,32,1536]{2,1,0:T(8,128)(2,1)S(1)}, u32[]{:S(2)}, u32[]{:S(2)}) async-start(f16[8,32,1536]{2,1,0:T(8,128)(2,1)} %bitcast.23), calls=%async_computation.1 | async-start | bytes 1572864 | tf_op jit(solution)/shard_map/all_to_all | solution.py:228
  38.1 25.9 %copy-start.6 = (s32[6,8]{1,0:T(8,128)S(1)}, s32[6,8]{1,0:T(8,128)}, u32[]{:S(2)}) copy-start(s32[6,8]{1,0:T(8,128)} %param.12) | copy-start | bytes 580
  38.1 36.0 %copy-start.7 = (s32[3,8]{1,0:T(4,128)S(1)}, s32[3,8]{1,0:T(4,128)}, u32[]{:S(2)}) copy-start(s32[3,8]{1,0:T(4,128)} %param.14) | copy-start | bytes 292
  41.6 9.5 %collective-permute-start.2 = (bf16[192,256]{1,0:T(8,128)(2,1)}, bf16[192,256]{1,0:T(8,128)(2,1)S(1)}, u32[]{:S(2)}, u32[]{:S(2)}) collective-permute-start(bf16[192,256]{1,0:T(8,128)(2,1)} %get-tuple-element.15), channel_id=1, source_target_pairs={{0,8},{8,16},{16,24},{24,32},{32,40},{40,48},{48,56},{56,64},{64,7... | collective-permute-start | bytes 294920 | tf_op jit(solution)/shard_map/ppermute | solution.py:235
  44.8 7.4 %collective-permute-start.3 = (bf16[192,256]{1,0:T(8,128)(2,1)}, bf16[192,256]{1,0:T(8,128)(2,1)S(1)}, u32[]{:S(2)}, u32[]{:S(2)}) collective-permute-start(bf16[192,256]{1,0:T(8,128)(2,1)} %get-tuple-element.15), channel_id=1, source_target_pairs={{0,504},{8,0},{16,8},{24,16},{32,24},{40,32},{48,40},{56,48},{64,5... | collective-permute-start | bytes 294920 | tf_op jit(solution)/shard_map/ppermute | solution.py:235
  52.2 33.0 %copy-start.1 = (bf16[576,256]{1,0:T(8,128)(2,1)}, bf16[576,256]{1,0:T(8,128)(2,1)S(1)}, u32[]{:S(2)}) copy-start(bf16[576,256]{1,0:T(8,128)(2,1)S(1)} %constant_dynamic-update-slice_fusion.refs_1_) | copy-start | bytes 884740
  52.2 32.9 %collective-permute-start.4 = (bf16[576,256]{1,0:T(8,128)(2,1)S(1)}, bf16[576,256]{1,0:T(8,128)(2,1)S(1)}, u32[]{:S(2)}, u32[]{:S(2)}) collective-permute-start(bf16[576,256]{1,0:T(8,128)(2,1)S(1)} %constant_dynamic-update-slice_fusion.refs_1_), channel_id=1, source_target_pairs={{0,24},{8,32},{16,40},{24,48},{32,56},{40,64},{48,72},{56,80},{64,... | collective-permute-start | bytes 884744 | tf_op jit(solution)/shard_map/ppermute | solution.py:235
  54.5 30.6 %collective-permute-start.5 = (bf16[576,256]{1,0:T(8,128)(2,1)S(1)}, bf16[576,256]{1,0:T(8,128)(2,1)S(1)}, u32[]{:S(2)}, u32[]{:S(2)}) collective-permute-start(bf16[576,256]{1,0:T(8,128)(2,1)S(1)} %constant_dynamic-update-slice_fusion.refs_1_), channel_id=1, source_target_pairs={{0,488},{8,496},{16,504},{24,0},{32,8},{40,16},{48,24},{56,32},{64... | collective-permute-start | bytes 884744 | tf_op jit(solution)/shard_map/ppermute | solution.py:235
  64.7 10.5 %collective-permute-start = (bf16[384,256]{1,0:T(8,128)(2,1)}, bf16[384,256]{1,0:T(8,128)(2,1)S(1)}, u32[]{:S(2)}, u32[]{:S(2)}) collective-permute-start(bf16[384,256]{1,0:T(8,128)(2,1)} %get-tuple-element.13.refs_1_), channel_id=1, source_target_pairs={{0,1},{1,2},{2,3},{3,4},{4,5},{5,6},{6,7},{7,8},{8,9},{9,10},{10,1... | collective-permute-start | bytes 589832 | tf_op jit(solution)/shard_map/ppermute | solution.py:235
  72.2 9.3 %collective-permute-start.1 = (bf16[384,256]{1,0:T(8,128)(2,1)}, bf16[384,256]{1,0:T(8,128)(2,1)S(1)}, u32[]{:S(2)}, u32[]{:S(2)}) collective-permute-start(bf16[384,256]{1,0:T(8,128)(2,1)} %get-tuple-element.13.refs_1_), channel_id=1, source_target_pairs={{0,511},{1,0},{2,1},{3,2},{4,3},{5,4},{6,5},{7,6},{8,7},{9,8},{10,... | collective-permute-start | bytes 589832 | tf_op jit(solution)/shard_map/ppermute | solution.py:235
  75.1 6.4 %copy-start.4 = (bf16[384,256]{1,0:T(8,128)(2,1)}, bf16[384,256]{1,0:T(8,128)(2,1)S(1)}, u32[]{:S(2)}) copy-start(bf16[384,256]{1,0:T(8,128)(2,1)S(1)} %collective-permute-done.refs_0_) | copy-start | bytes 589828
  81.5 0.7 copy-start.5
  85.1 0.7 copy-start.2
  85.1 0.8 copy-start.3
where the time goes:
time: 88.9 us; the launch traced here: 88.4 us
  starting transfers between devices  40.9 us (46%)
  Pallas kernels  19.4 us (22%)
  waiting for transfers between devices  17.3 us (19%)
  other arithmetic  5.66 us (6%)
  local copies, waits for them, and re-layouts  4.43 us (5%)
    ppermute x6, starting transfers between devices, shifted(): return lax.ppermute(array, axis, pairs)  29.8 us
    all_to_all x2, starting transfers between devices, gathered(): got = lax.all_to_all(sent, 'samp', split_axis=0, concat_axis=0, tiled=True)  11.1 us
    pallas_call x1, Pallas kernels, run_compress(): pl.pallas_call(compress, out_shape=(jax.ShapeDtypeStruct((RANK, y.shape[1...  10.5 us
    all_to_all x2, waiting for transfers between devices, gathered(): got = lax.all_to_all(sent, 'samp', split_axis=0, concat_axis=0, tiled=True)  9.33 us
    ppermute x6, waiting for transfers between devices, shifted(): return lax.ppermute(array, axis, pairs)  7.92 us
    pallas_call x2, Pallas kernels, run_couple(): pl.pallas_call(couple, out_shape=jax.ShapeDtypeStruct((rows * 4 * RANK, 1...  5.34 us
    pallas_call x1, Pallas kernels, run_project(): pl.pallas_call(project, out_shape=(jax.ShapeDtypeStruct((owned * RANK, sa...  3.52 us
    mul x2, other arithmetic, gathered(): got.astype(f32).reshape(rows * devices, columns // devices) * (1.0 / SCALE)  2.8 us
  transfers between devices with their start and end apart: 8, of which 5 were waited for; matrix products, arithmetic and copies ran while one was open for 5% of the time, Pallas kernels for 15%

commit v1 on v0

--- a/solution.py
+++ b/solution.py
@@ -5,6 +5,7 @@
 from jax.experimental import pallas as pl
 from jax.experimental.pallas import tpu as pltpu
 from jax.sharding import PartitionSpec as P
+
 
 f32 = jnp.float32
 bf16 = jnp.bfloat16
@@ -142,7 +143,7 @@
         b_ref[RANK * p : RANK * p + RANK, :] = product(split(transfer_ref[p]), stack, (1, 0)).astype(bf16)
 
 
-def couple(far_ref, count_ref, left_ref, *refs):
+def couple(place, far_ref, count_ref, left_ref, *refs):
     pieces, out_ref, table = refs[:-2], refs[-2], refs[-1]
     rows = left_ref.shape[0] // RANK
     slots = far_ref.shape[1]
@@ -156,10 +157,11 @@
     low = lane < RANK
     samples = left_ref.shape[1]
     dims = (((1,), (1,)), ((), ()))
+    spot = place()
     for i in range(rows):
         left = left_ref[RANK * i : RANK * i + RANK, :]
         for k in range(0, slots, 2):
-            right = jnp.concatenate([table[far_ref[i, k + e]] for e in range(2)], axis=0)
+            right = jnp.concatenate([table[jnp.clip(spot(far_ref[i, k + e]), 0, at - 1)] for e in range(2)], axis=0)
             x = lax.dot_general(left, right, dims, preferred_element_type=f32)
             even, odd = x[: RANK // 2], x[RANK // 2 :]
             first = jnp.where(low, even, pltpu.roll(odd, RANK, 1))
@@ -171,6 +173,11 @@
 
 vmem = pl.BlockSpec(memory_space=pltpu.VMEM)
 smem = pl.BlockSpec(memory_space=pltpu.SMEM)
+params = pltpu.CompilerParams(vmem_limit_bytes=16 << 20)
+
+
+def cost(us):
+    return pl.CostEstimate(flops=us * 10**9, bytes_accessed=us * 10**6, transcendentals=0)
 
 
 def run_compress(y, test, ptest):
@@ -187,6 +194,8 @@
         in_specs=[vmem] * 3,
         out_specs=(vmem,) * 4,
         scratch_shapes=[pltpu.VMEM((owned * RANK, 128), f32)] * (samples // 128),
+        compiler_params=params,
+        cost_estimate=cost(12),
         name="compress",
     )(y, test, ptest)
 
@@ -202,20 +211,23 @@
         ),
         in_specs=[vmem] * 3,
         out_specs=(vmem,) * 2,
+        compiler_params=params,
+        cost_estimate=cost(4),
         name="project",
     )(o, basis, transfer)
 
 
-def run_couple(far, count, left, pieces, name):
+def run_couple(place, far, count, left, pieces):
     rows, slots = far.shape
     total = sum(p.shape[0] for p in pieces) // RANK
     out = pl.pallas_call(
-        couple,
+        functools.partial(couple, place),
         out_shape=jax.ShapeDtypeStruct((rows * 4 * RANK, 128), f32),
         in_specs=[smem, smem, vmem] + [vmem] * len(pieces),
         out_specs=vmem,
         scratch_shapes=[pltpu.VMEM((total, RANK, left.shape[1]), bf16)],
-        name=name,
+        compiler_params=params,
+        cost_estimate=cost(3),
     )(far, count, left, *pieces)
     out = out.reshape(rows, RANK // 2, slots, 128)
     return out.transpose(0, 2, 1, 3).reshape(rows, slots, RANK * RANK)
@@ -229,30 +241,75 @@
     return got.astype(f32).reshape(rows * devices, columns // devices) * (1.0 / SCALE)
 
 
-def shifted(array, axis, by):
-    devices = lax.axis_size(axis)
-    pairs = [(i, (i - by) % devices) for i in range(devices)]
-    return lax.ppermute(array, axis, pairs)
+def neighbours(size):
+    up = [(i, i + 1) for i in range(size - 1)]
+    return up, [(j, i) for i, j in up]
+
+
+def far_pairs(rows):
+    first, second = [], []
+    for start in range(3):
+        chain = list(range(start, rows, 3))
+        for at, (i, j) in enumerate(zip(chain, chain[1:])):
+            if start == 0:
+                first.append((i, j))
+                second.append((j, i))
+            else:
+                (second if at % 2 else first).extend([(i, j), (j, i)])
+    second.append((0, 2))
+    first.append((rows - 1, rows - 3))
+    got = [[{r}, {r}] for r in range(rows)]
+    for pairs in (first, second):
+        assert len({i for i, _ in pairs}) == len({j for _, j in pairs}) == len(pairs)
+        for i, j in pairs:
+            got[j][1] |= {i - 1, i, i + 1}
+    for r in range(rows):
+        have = got[r][1] | {r - 1, r + 1}
+        assert all(q in have for q in range(max(r - REACH, 0), min(r + REACH + 1, rows)))
+    return first, second
 
 
 def body(sketch, probes, test_leaf, test_parent, leaf_far, leaf_count, parent_far, parent_count):
     owned = leaf_far.shape[0]
     per_device = parent_far.shape[0]
+    row_count = lax.axis_size("rows")
+    samp_count = lax.axis_size("samp")
     y = gathered(sketch)
     o = gathered(probes)
     basis, w, transfer, a = run_compress(y, test_leaf, test_parent)
     v, b = run_project(o, basis, transfer)
-    before, after = shifted(b, "rows", -1), shifted(b, "rows", 1)
-    near = jnp.concatenate([before, b, after], axis=0)
-    v_before, v_after = shifted(v, ("rows", "samp"), -1), shifted(v, ("rows", "samp"), 1)
-    far_before, far_after = shifted(near, "rows", -3), shifted(near, "rows", 3)
-    first_leaf = lax.axis_index(("rows", "samp")) * owned
-    leaf_at = jnp.clip(leaf_far - first_leaf + owned, 0, 3 * owned - 1)
-    leaf_coupling = run_couple(leaf_at, leaf_count, w, [v_before, v, v_after], "leaf")
-    row = parent_far // (per_device * lax.axis_size("samp"))
-    step = row - lax.axis_index("rows") + REACH
-    parent_at = jnp.clip(step * per_device + parent_far % per_device, 0, (2 * REACH + 1) * per_device - 1)
-    parent_coupling = run_couple(parent_at, parent_count, a, [far_before, near, far_after], "parent")
+    up, down = neighbours(row_count)
+    near = [lax.ppermute(b, "rows", up), b, lax.ppermute(b, "rows", down)]
+    near = jnp.concatenate(near, axis=0)
+    both = ("rows", "samp")
+    up, down = neighbours(lax.axis_size(both))
+    halo = [lax.ppermute(v, both, up), v, lax.ppermute(v, both, down)]
+    pairs = far_pairs(row_count)
+    far = [lax.ppermute(near, "rows", pairs[e]) for e in range(2)]
+
+    def leaf_place():
+        before = lax.axis_index(both) * owned - owned
+        return lambda leaf: leaf - before
+
+    def parent_place():
+        row = lax.axis_index("rows")
+        ahead = lax.rem(row, 6)
+        one = jnp.where((ahead == 0) | (ahead == 3) | (ahead == 4) | (ahead == 5), -REACH + 1, REACH - 1)
+        one = jnp.where(row == row_count - 3, 2, one)
+        two = jnp.where((ahead == 1) | (ahead == 2), -REACH + 1, REACH - 1)
+        two = jnp.where(row == 2, -2, two)
+        across = per_device * samp_count
+
+        def spot(parent):
+            away = lax.div(parent, across) - row
+            far_at = jnp.where(abs(away - one) <= 1, away - one + 4, away - two + 7)
+            at = jnp.where(abs(away) <= 1, away + 1, far_at)
+            return at * per_device + lax.rem(parent, per_device)
+
+        return spot
+
+    leaf_coupling = run_couple(leaf_place, leaf_far, leaf_count, w, halo)
+    parent_coupling = run_couple(parent_place, parent_far, parent_count, a, [near, *far])
     return (basis, leaf_coupling, transfer, parent_coupling)
 
 

time: 88.9 us -> 75.5 us (0.85)
  the two profiles are of different devices: /device:TPU:27 before, /device:TPU:4 now
where the time goes in v1:
time: 75.5 us; the launch traced here: 75 us
  starting transfers between devices  27.9 us (37%)
  waiting for transfers between devices  27.1 us (36%)
  Pallas kernels  14.4 us (19%)
  local copies, waits for them, and re-layouts  2.74 us (4%)
  other arithmetic  2.07 us (3%)
  between operations  0.85 us (1%)
    all_to_all x2, waiting for transfers between devices, gathered(): got = lax.all_to_all(sent, 'samp', split_axis=0, concat_axis=0, tiled=True)  15.2 us
    ppermute x2, waiting for transfers between devices, body(): halo = [lax.ppermute(v, both, up), v, lax.ppermute(v, both, down)]  11.9 us
    pallas_call x1, Pallas kernels, run_compress(): pl.pallas_call(compress, out_shape=(jax.ShapeDtypeStruct((RANK, y.shape[1...  8.98 us
    all_to_all x2, starting transfers between devices, gathered(): got = lax.all_to_all(sent, 'samp', split_axis=0, concat_axis=0, tiled=True)  8.02 us
    ppermute x2, starting transfers between devices, body(): far = [lax.ppermute(near, 'rows', pairs[e]) for e in range(2)]  7.82 us
    ppermute x2, starting transfers between devices, body(): halo = [lax.ppermute(v, both, up), v, lax.ppermute(v, both, down)]  6.21 us
    ppermute x2, starting transfers between devices, body(): near = [lax.ppermute(b, 'rows', up), b, lax.ppermute(b, 'rows', down)]  5.84 us
    pallas_call x2, Pallas kernels, run_couple(): pl.pallas_call(functools.partial(couple, place), out_shape=jax.ShapeDtype...  4.12 us
  transfers between devices with their start and end apart: 8, of which 3 were waited for; matrix products, arithmetic and copies ran while one was open for 2% of the time, Pallas kernels for 15%

profile of v1, /device:TPU:4, one launch (start us, length us, event | category | flops | bytes accessed | tf_op | source)
XLA Modules:
  0.0 75.0 jit_solution(471617331269600711)
XLA Ops:
  0.6 1.5 %multiply_convert_fusion.1 = f16[32,12288]{1,0:T(8,128)(2,1)S(1)} fusion(f32[32,12288]{1,0:T(8,128)} %param.8), kind=kLoop, calls=%fused_computation.3 | loop fusion | flops 786432 | bytes 2359296 | tf_op jit(solution)/shard_map/convert_element_type | solution.py:239
  2.2 0.0 copy-start.8
  2.2 1.0 %copy.19 = f16[4,8,8,1536]{3,2,0,1:T(8,128)(2,1)} copy(f16[4,8,8,1536]{3,2,1,0:T(8,128)(2,1)S(1)} %bitcast.28) | data formatting | bytes 1572864 | tf_op jit(solution)/shard_map/reshape | solution.py:239
  3.2 4.5 %all-to-all-start = ((f16[8,32,1536]{2,1,0:T(8,128)(2,1)}), f16[8,32,1536]{2,1,0:T(8,128)(2,1)S(1)}, u32[]{:S(2)}, u32[]{:S(2)}) async-start(f16[8,32,1536]{2,1,0:T(8,128)(2,1)} %bitcast.25), calls=%async_computation | async-start | bytes 1572864 | tf_op jit(solution)/shard_map/all_to_all | solution.py:240
  7.7 0.0 copy-done.8
  7.7 0.1 multiply_convert_fusion
  7.8 1.0 %copy.18 = f16[4,8,8,1536]{3,2,0,1:T(8,128)(2,1)} copy(f16[4,8,8,1536]{3,2,1,0:T(8,128)(2,1)S(1)} %bitcast.29) | data formatting | bytes 1572864 | tf_op jit(solution)/shard_map/reshape | solution.py:239
  8.8 12.0 %all-to-all-done = f16[8,32,1536]{2,1,0:T(8,128)(2,1)S(1)} async-done(((f16[8,32,1536]{2,1,0:T(8,128)(2,1)}), f16[8,32,1536]{2,1,0:T(8,128)(2,1)S(1)}, u32[]{:S(2)}, u32[]{:S(2)}) %all-to-all-start) | async-done | bytes 786464 | tf_op jit(solution)/shard_map/all_to_all | solution.py:240
  20.8 3.5 %all-to-all-start.1 = ((f16[8,32,1536]{2,1,0:T(8,128)(2,1)}), f16[8,32,1536]{2,1,0:T(8,128)(2,1)S(1)}, u32[]{:S(2)}, u32[]{:S(2)}) async-start(f16[8,32,1536]{2,1,0:T(8,128)(2,1)} %bitcast.23), calls=%async_computation.1 | async-start | bytes 1572864 | tf_op jit(solution)/shard_map/all_to_all | solution.py:240
  24.3 0.0 copy-start
  24.4 0.0 copy-start.1
  24.4 0.2 convert_multiply_fusion.1
  24.6 0.6 copy-done
  25.2 0.0 copy-done.1
  25.2 9.0 %compress.1 = (f32[64,1536]{1,0:T(8,128)}, bf16[384,256]{1,0:T(8,128)(2,1)S(1)}, f32[3,64,128]{2,1,0:T(8,128)}, bf16[192,256]{1,0:T(8,128)(2,1)S(1)}) custom-call(f32[256,1536]{1,0:T(8,128)S(1)} %bitcast.26, f32[64,256]{1,0:T(8,128)S(1)} %copy-done, f32[64,256]{1,0:T(8,128)S(1)} %copy-done.1), custom_call_target="tpu_custom_call" | custom-call | flops 12000000000 | bytes 12000000 | tf_op jit(solution)/shard_map/compress/pallas_call | solution.py:186
  34.2 0.0 copy-start.6
  34.2 0.0 copy-start.7
  34.2 3.2 %all-to-all-done.1 = f16[8,32,1536]{2,1,0:T(8,128)(2,1)S(1)} async-done(((f16[8,32,1536]{2,1,0:T(8,128)(2,1)}), f16[8,32,1536]{2,1,0:T(8,128)(2,1)S(1)}, u32[]{:S(2)}, u32[]{:S(2)}) %all-to-all-start.1) | async-done | bytes 786464 | tf_op jit(solution)/shard_map/all_to_all | solution.py:240
  37.4 0.2 convert_multiply_fusion
  37.6 0.0 copy-done.6
  37.6 0.0 copy-done.7
  37.6 0.0 copy-start.2
  37.6 0.0 copy-start.4
  37.6 1.3 %project.1 = (bf16[384,256]{1,0:T(8,128)(2,1)S(1)}, bf16[192,256]{1,0:T(8,128)(2,1)S(1)}) custom-call(f32[256,1536]{1,0:T(8,128)S(1)} %bitcast.27, f32[64,1536]{1,0:T(8,128)S(1)} %copy-done.6, f32[3,64,128]{2,1,0:T(8,128)S(1)} %copy-done.7), custom_call_target="tpu_custom_call" | custom-call | flops 4000000000 | bytes 4000000 | tf_op jit(solution)/shard_map/project/pallas_call | solution.py:206
  39.0 3.1 %collective-permute-start.2 = (bf16[192,256]{1,0:T(8,128)(2,1)S(1)}, bf16[192,256]{1,0:T(8,128)(2,1)S(1)}, u32[]{:S(2)}, u32[]{:S(2)}) collective-permute-start(bf16[192,256]{1,0:T(8,128)(2,1)S(1)} %get-tuple-element.15), channel_id=1, source_target_pairs={{0,8},{8,16},{16,24},{24,32},{32,40},{40,48},{48,56},{56,64},{64,7... | collective-permute-start | bytes 294920 | tf_op jit(solution)/shard_map/ppermute | solution.py:282
  42.1 2.7 %collective-permute-start.3 = (bf16[192,256]{1,0:T(8,128)(2,1)S(1)}, bf16[192,256]{1,0:T(8,128)(2,1)S(1)}, u32[]{:S(2)}, u32[]{:S(2)}) collective-permute-start(bf16[192,256]{1,0:T(8,128)(2,1)S(1)} %get-tuple-element.15), channel_id=1, source_target_pairs={{8,0},{16,8},{24,16},{32,24},{40,32},{48,40},{56,48},{64,56},{72,6... | collective-permute-start | bytes 294920 | tf_op jit(solution)/shard_map/ppermute | solution.py:282
  44.8 4.3 %collective-permute-start.1 = (bf16[384,256]{1,0:T(8,128)(2,1)S(1)}, bf16[384,256]{1,0:T(8,128)(2,1)S(1)}, u32[]{:S(2)}, u32[]{:S(2)}) collective-permute-start(bf16[384,256]{1,0:T(8,128)(2,1)S(1)} %get-tuple-element.13.refs_1_), channel_id=1, source_target_pairs={{1,0},{2,1},{3,2},{4,3},{5,4},{6,5},{7,6},{8,7},{9,8},{10,9},{11,1... | collective-permute-start | bytes 589832 | tf_op jit(solution)/shard_map/ppermute | solution.py:286
  49.1 1.9 %collective-permute-start = (bf16[384,256]{1,0:T(8,128)(2,1)S(1)}, bf16[384,256]{1,0:T(8,128)(2,1)S(1)}, u32[]{:S(2)}, u32[]{:S(2)}) collective-permute-start(bf16[384,256]{1,0:T(8,128)(2,1)S(1)} %get-tuple-element.13.refs_1_), channel_id=1, source_target_pairs={{0,1},{1,2},{2,3},{3,4},{4,5},{5,6},{6,7},{7,8},{8,9},{9,10},{10,1... | collective-permute-start | bytes 589832 | tf_op jit(solution)/shard_map/ppermute | solution.py:286
  51.1 0.0 collective-permute-done.2
  51.1 0.0 collective-permute-done.3
  51.1 1.3 %collective-permute-start.5 = (bf16[576,256]{1,0:T(8,128)(2,1)S(1)}, bf16[576,256]{1,0:T(8,128)(2,1)S(1)}, u32[]{:S(2)}, u32[]{:S(2)}) collective-permute-start(bf16[576,256]{1,0:T(8,128)(2,1)S(1)} %constant_dynamic-update-slice_fusion.refs_0_), channel_id=1, source_target_pairs={{24,0},{48,24},{72,48},{96,72},{120,96},{144,120},{168,144},{192,1... | collective-permute-start | bytes 884744 | tf_op jit(solution)/shard_map/ppermute | solution.py:288
  52.4 6.5 %collective-permute-start.4 = (bf16[576,256]{1,0:T(8,128)(2,1)S(1)}, bf16[576,256]{1,0:T(8,128)(2,1)S(1)}, u32[]{:S(2)}, u32[]{:S(2)}) collective-permute-start(bf16[576,256]{1,0:T(8,128)(2,1)S(1)} %constant_dynamic-update-slice_fusion.refs_0_), channel_id=1, source_target_pairs={{0,24},{24,48},{48,72},{72,96},{96,120},{120,144},{144,168},{168,1... | collective-permute-start | bytes 884744 | tf_op jit(solution)/shard_map/ppermute | solution.py:288
  59.0 0.0 collective-permute-done.1.refs_2_
  59.0 11.9 %collective-permute-done.refs_0_ = bf16[384,256]{1,0:T(8,128)(2,1)S(1)} collective-permute-done((bf16[384,256]{1,0:T(8,128)(2,1)S(1)}, bf16[384,256]{1,0:T(8,128)(2,1)S(1)}, u32[]{:S(2)}, u32[]{:S(2)}) %collective-permute-start) | collective-permute-done | bytes 196640 | tf_op jit(solution)/shard_map/ppermute | solution.py:286
  70.9 0.0 copy-done.2
  70.9 0.0 copy-done.4
  70.9 0.0 copy-start.3
  70.9 0.0 copy-start.5
  70.9 2.3 %shard_map.111 = f32[1536,128]{1,0:T(8,128)} custom-call(s32[6,8]{1,0:T(8,128)S(1)} %copy-done.2, s32[6]{0:T(128)S(1)} %copy-done.4, bf16[384,256]{1,0:T(8,128)(2,1)S(1)} %get-tuple-element.11.left_ref, bf16[384,256]{1,0:T(8,128)(2,1)S(1)} %collective-permute-done.refs_0_, bf16[384,256]{1,0:T(8,128)(2,1)S(1)} %get-tuple-element.13.refs_1_, ...), custom_call_target="tpu_custom_call" | custom-call | flops 3000000000 | bytes 3000000 | tf_op jit(solution)/shard_map/pallas_call | solution.py:223
  73.1 0.0 collective-permute-done.5.refs_2_
  73.1 0.0 collective-permute-done.4.refs_1_
  73.1 0.0 copy-done.3
  73.1 0.0 copy-done.5
  73.2 1.9 %shard_map.112 = f32[768,128]{1,0:T(8,128)} custom-call(s32[3,8]{1,0:T(4,128)S(1)} %copy-done.3, s32[3]{0:T(128)S(1)} %copy-done.5, bf16[192,256]{1,0:T(8,128)(2,1)S(1)} %get-tuple-element.14.left_ref, bf16[576,256]{1,0:T(8,128)(2,1)S(1)} %constant_dynamic-update-slice_fusion.refs_0_, bf16[576,256]{1,0:T(8,128)(2,1)S(1)} %collective-permute-done.4.refs_1_, ...), custom_call_target="tpu_custom_call" | custom-call | flops 3000000000 | bytes 3000000 | tf_op jit(solution)/shard_map/pallas_call | solution.py:223
  (3 shorter events, 0.0 us)
Async XLA Ops:
  2.2 5.5 %copy-start.8 = (f32[32,12288]{1,0:T(8,128)S(1)}, f32[32,12288]{1,0:T(8,128)}, u32[]{:S(2)}) copy-start(f32[32,12288]{1,0:T(8,128)} %param.9) | copy-start | bytes 4718596
  3.2 17.6 %all-to-all-start = ((f16[8,32,1536]{2,1,0:T(8,128)(2,1)}), f16[8,32,1536]{2,1,0:T(8,128)(2,1)S(1)}, u32[]{:S(2)}, u32[]{:S(2)}) async-start(f16[8,32,1536]{2,1,0:T(8,128)(2,1)} %bitcast.25), calls=%async_computation | async-start | bytes 1572864 | tf_op jit(solution)/shard_map/all_to_all | solution.py:240
  20.8 16.6 %all-to-all-start.1 = ((f16[8,32,1536]{2,1,0:T(8,128)(2,1)}), f16[8,32,1536]{2,1,0:T(8,128)(2,1)S(1)}, u32[]{:S(2)}, u32[]{:S(2)}) async-start(f16[8,32,1536]{2,1,0:T(8,128)(2,1)} %bitcast.23), calls=%async_computation.1 | async-start | bytes 1572864 | tf_op jit(solution)/shard_map/all_to_all | solution.py:240
  24.3 0.8 %copy-start = (f32[64,256]{1,0:T(8,128)S(1)}, f32[64,256]{1,0:T(8,128)}, u32[]{:S(2)}) copy-start(f32[64,256]{1,0:T(8,128)} %test_ref.1) | copy-start | bytes 196612
  24.4 0.9 %copy-start.1 = (f32[64,256]{1,0:T(8,128)S(1)}, f32[64,256]{1,0:T(8,128)}, u32[]{:S(2)}) copy-start(f32[64,256]{1,0:T(8,128)} %ptest_ref.1) | copy-start | bytes 196612
  34.2 3.4 %copy-start.6 = (f32[64,1536]{1,0:T(8,128)S(1)}, f32[64,1536]{1,0:T(8,128)}, u32[]{:S(2)}) copy-start(f32[64,1536]{1,0:T(8,128)} %get-tuple-element.6.basis_ref) | copy-start | bytes 1179652
  34.2 3.4 %copy-start.7 = (f32[3,64,128]{2,1,0:T(8,128)S(1)}, f32[3,64,128]{2,1,0:T(8,128)}, u32[]{:S(2)}) copy-start(f32[3,64,128]{2,1,0:T(8,128)} %get-tuple-element.8.transfer_ref) | copy-start | bytes 294916
  37.6 33.2 %copy-start.2 = (s32[6,8]{1,0:T(8,128)S(1)}, s32[6,8]{1,0:T(8,128)}, u32[]{:S(2)}) copy-start(s32[6,8]{1,0:T(8,128)} %far_ref.2) | copy-start | bytes 580
  37.6 33.2 %copy-start.4 = (s32[6]{0:T(128)S(1)}, s32[6]{0:T(128)}, u32[]{:S(2)}) copy-start(s32[6]{0:T(128)} %count_ref.2) | copy-start | bytes 76
  39.0 12.1 %collective-permute-start.2 = (bf16[192,256]{1,0:T(8,128)(2,1)S(1)}, bf16[192,256]{1,0:T(8,128)(2,1)S(1)}, u32[]{:S(2)}, u32[]{:S(2)}) collective-permute-start(bf16[192,256]{1,0:T(8,128)(2,1)S(1)} %get-tuple-element.15), channel_id=1, source_target_pairs={{0,8},{8,16},{16,24},{24,32},{32,40},{40,48},{48,56},{56,64},{64,7... | collective-permute-start | bytes 294920 | tf_op jit(solution)/shard_map/ppermute | solution.py:282
  42.1 9.0 %collective-permute-start.3 = (bf16[192,256]{1,0:T(8,128)(2,1)S(1)}, bf16[192,256]{1,0:T(8,128)(2,1)S(1)}, u32[]{:S(2)}, u32[]{:S(2)}) collective-permute-start(bf16[192,256]{1,0:T(8,128)(2,1)S(1)} %get-tuple-element.15), channel_id=1, source_target_pairs={{8,0},{16,8},{24,16},{32,24},{40,32},{48,40},{56,48},{64,56},{72,6... | collective-permute-start | bytes 294920 | tf_op jit(solution)/shard_map/ppermute | solution.py:282
  44.8 14.1 %collective-permute-start.1 = (bf16[384,256]{1,0:T(8,128)(2,1)S(1)}, bf16[384,256]{1,0:T(8,128)(2,1)S(1)}, u32[]{:S(2)}, u32[]{:S(2)}) collective-permute-start(bf16[384,256]{1,0:T(8,128)(2,1)S(1)} %get-tuple-element.13.refs_1_), channel_id=1, source_target_pairs={{1,0},{2,1},{3,2},{4,3},{5,4},{6,5},{7,6},{8,7},{9,8},{10,9},{11,1... | collective-permute-start | bytes 589832 | tf_op jit(solution)/shard_map/ppermute | solution.py:286
  49.1 21.7 %collective-permute-start = (bf16[384,256]{1,0:T(8,128)(2,1)S(1)}, bf16[384,256]{1,0:T(8,128)(2,1)S(1)}, u32[]{:S(2)}, u32[]{:S(2)}) collective-permute-start(bf16[384,256]{1,0:T(8,128)(2,1)S(1)} %get-tuple-element.13.refs_1_), channel_id=1, source_target_pairs={{0,1},{1,2},{2,3},{3,4},{4,5},{5,6},{6,7},{7,8},{8,9},{9,10},{10,1... | collective-permute-start | bytes 589832 | tf_op jit(solution)/shard_map/ppermute | solution.py:286
  51.1 22.0 %collective-permute-start.5 = (bf16[576,256]{1,0:T(8,128)(2,1)S(1)}, bf16[576,256]{1,0:T(8,128)(2,1)S(1)}, u32[]{:S(2)}, u32[]{:S(2)}) collective-permute-start(bf16[576,256]{1,0:T(8,128)(2,1)S(1)} %constant_dynamic-update-slice_fusion.refs_0_), channel_id=1, source_target_pairs={{24,0},{48,24},{72,48},{96,72},{120,96},{144,120},{168,144},{192,1... | collective-permute-start | bytes 884744 | tf_op jit(solution)/shard_map/ppermute | solution.py:288
  52.4 20.7 %collective-permute-start.4 = (bf16[576,256]{1,0:T(8,128)(2,1)S(1)}, bf16[576,256]{1,0:T(8,128)(2,1)S(1)}, u32[]{:S(2)}, u32[]{:S(2)}) collective-permute-start(bf16[576,256]{1,0:T(8,128)(2,1)S(1)} %constant_dynamic-update-slice_fusion.refs_0_), channel_id=1, source_target_pairs={{0,24},{24,48},{48,72},{72,96},{96,120},{120,144},{144,168},{168,1... | collective-permute-start | bytes 884744 | tf_op jit(solution)/shard_map/ppermute | solution.py:288
  70.9 2.3 %copy-start.3 = (s32[3,8]{1,0:T(4,128)S(1)}, s32[3,8]{1,0:T(4,128)}, u32[]{:S(2)}) copy-start(s32[3,8]{1,0:T(4,128)} %far_ref.3) | copy-start | bytes 292
  70.9 2.3 %copy-start.5 = (s32[3]{0:T(128)S(1)}, s32[3]{0:T(128)}, u32[]{:S(2)}) copy-start(s32[3]{0:T(128)} %count_ref.3) | copy-start | bytes 40

commit v2 on v1

--- a/solution.py
+++ b/solution.py
@@ -241,32 +241,32 @@
     return got.astype(f32).reshape(rows * devices, columns // devices) * (1.0 / SCALE)
 
 
-def neighbours(size):
-    up = [(i, i + 1) for i in range(size - 1)]
-    return up, [(j, i) for i, j in up]
+def swaps(chain, late):
+    found = []
+    for i, j in list(zip(chain, chain[1:]))[late::2]:
+        found += [(i, j), (j, i)]
+    return found
+
+
+def near_pairs(size):
+    return swaps(range(size), 0), swaps(range(size), 1)
 
 
 def far_pairs(rows):
-    first, second = [], []
+    sets = [[], []]
     for start in range(3):
-        chain = list(range(start, rows, 3))
-        for at, (i, j) in enumerate(zip(chain, chain[1:])):
-            if start == 0:
-                first.append((i, j))
-                second.append((j, i))
-            else:
-                (second if at % 2 else first).extend([(i, j), (j, i)])
-    second.append((0, 2))
-    first.append((rows - 1, rows - 3))
-    got = [[{r}, {r}] for r in range(rows)]
-    for pairs in (first, second):
+        for late in range(2):
+            sets[late ^ (start == 1)] += swaps(range(start, rows, 3), late)
+    sets[1] += [(0, 2), (rows - 1, rows - 3)]
+    got = [{r} for r in range(rows)]
+    for pairs in sets:
         assert len({i for i, _ in pairs}) == len({j for _, j in pairs}) == len(pairs)
         for i, j in pairs:
-            got[j][1] |= {i - 1, i, i + 1}
+            got[j] |= {i - 1, i, i + 1}
     for r in range(rows):
-        have = got[r][1] | {r - 1, r + 1}
+        have = got[r] | {r - 1, r + 1}
         assert all(q in have for q in range(max(r - REACH, 0), min(r + REACH + 1, rows)))
-    return first, second
+    return sets
 
 
 def body(sketch, probes, test_leaf, test_parent, leaf_far, leaf_count, parent_far, parent_count):
@@ -278,32 +278,48 @@
     o = gathered(probes)
     basis, w, transfer, a = run_compress(y, test_leaf, test_parent)
     v, b = run_project(o, basis, transfer)
-    up, down = neighbours(row_count)
-    near = [lax.ppermute(b, "rows", up), b, lax.ppermute(b, "rows", down)]
+    pairs = near_pairs(row_count)
+    near = [b] + [lax.ppermute(b, "rows", pairs[e]) for e in range(2)]
     near = jnp.concatenate(near, axis=0)
     both = ("rows", "samp")
-    up, down = neighbours(lax.axis_size(both))
-    halo = [lax.ppermute(v, both, up), v, lax.ppermute(v, both, down)]
+    pairs = near_pairs(row_count * samp_count)
+    halo = [v] + [lax.ppermute(v, both, pairs[e]) for e in range(2)]
     pairs = far_pairs(row_count)
     far = [lax.ppermute(near, "rows", pairs[e]) for e in range(2)]
 
     def leaf_place():
-        before = lax.axis_index(both) * owned - owned
-        return lambda leaf: leaf - before
+        own = lax.axis_index(both)
+        first = own * owned
+        odd = lax.rem(own, 2)
+
+        def spot(leaf):
+            later = (leaf >= first + owned).astype(jnp.int32)
+            earlier = (leaf < first).astype(jnp.int32)
+            piece = later * (1 + odd) + earlier * (2 - odd)
+            return leaf - first + (earlier - later + piece) * owned
+
+        return spot
 
     def parent_place():
         row = lax.axis_index("rows")
-        ahead = lax.rem(row, 6)
-        one = jnp.where((ahead == 0) | (ahead == 3) | (ahead == 4) | (ahead == 5), -REACH + 1, REACH - 1)
-        one = jnp.where(row == row_count - 3, 2, one)
-        two = jnp.where((ahead == 1) | (ahead == 2), -REACH + 1, REACH - 1)
+        odd = lax.rem(row, 2)
+        start = lax.rem(row, 3)
+        behind = (lax.rem(lax.div(row, 3), 2) == 1) != (start == 1)
+        one = jnp.where(behind, -(REACH - 1), REACH - 1)
+        two = -one
         two = jnp.where(row == 2, -2, two)
+        two = jnp.where(row == row_count - 3, 2, two)
         across = per_device * samp_count
 
         def spot(parent):
             away = lax.div(parent, across) - row
-            far_at = jnp.where(abs(away - one) <= 1, away - one + 4, away - two + 7)
-            at = jnp.where(abs(away) <= 1, away + 1, far_at)
+
+            def among(there, centre):
+                odd_there = lax.rem(row + centre + 2 * REACH, 2)
+                return jnp.where(there == 0, 0, jnp.where((there == 1) == (odd_there == 0), 1, 2))
+
+            far_at = jnp.where(abs(away - one) <= 1, 3 + among(away - one, one), 6 + among(away - two, two))
+            at = jnp.where(abs(away) <= 1, among(away, 0), far_at)
             return at * per_device + lax.rem(parent, per_device)
 
         return spot

time: 75.5 us -> 74.4 us (0.985)
  the two profiles are of different devices: /device:TPU:4 before, /device:TPU:5 now
where the time goes in v2:
time: 74.4 us; the launch traced here: 73.9 us
  starting transfers between devices  28.9 us (39%)
  waiting for transfers between devices  24.7 us (33%)
  Pallas kernels  14.6 us (20%)
  local copies, waits for them, and re-layouts  2.76 us (4%)
  other arithmetic  2.07 us (3%)
  between operations  0.85 us (1%)
    all_to_all x2, waiting for transfers between devices, gathered(): got = lax.all_to_all(sent, 'samp', split_axis=0, concat_axis=0, tiled=True)  13.3 us
    ppermute x2, waiting for transfers between devices, body(): far = [lax.ppermute(near, 'rows', pairs[e]) for e in range(2)]  11.3 us
    all_to_all x2, starting transfers between devices, gathered(): got = lax.all_to_all(sent, 'samp', split_axis=0, concat_axis=0, tiled=True)  9.56 us
    pallas_call x1, Pallas kernels, run_compress(): pl.pallas_call(compress, out_shape=(jax.ShapeDtypeStruct((RANK, y.shape[1...  8.98 us
    ppermute x2, starting transfers between devices, body(): far = [lax.ppermute(near, 'rows', pairs[e]) for e in range(2)]  7 us
    ppermute x2, starting transfers between devices, body(): near = [b] + [lax.ppermute(b, 'rows', pairs[e]) for e in range(2)]  6.29 us
    ppermute x2, starting transfers between devices, body(): halo = [v] + [lax.ppermute(v, both, pairs[e]) for e in range(2)]  6.09 us
    pallas_call x2, Pallas kernels, run_couple(): pl.pallas_call(functools.partial(couple, place), out_shape=jax.ShapeDtype...  4.32 us
  transfers between devices with their start and end apart: 8, of which 3 were waited for; matrix products, arithmetic and copies ran while one was open for 2% of the time, Pallas kernels for 15%

profile of v2, /device:TPU:5, one launch (start us, length us, event | category | flops | bytes accessed | tf_op | source)
XLA Modules:
  0.0 73.9 jit_solution(12708582071047778395)
XLA Ops:
  0.6 1.5 %multiply_convert_fusion.1 = f16[32,12288]{1,0:T(8,128)(2,1)S(1)} fusion(f32[32,12288]{1,0:T(8,128)} %param.8), kind=kLoop, calls=%fused_computation.3 | loop fusion | flops 786432 | bytes 2359296 | tf_op jit(solution)/shard_map/convert_element_type | solution.py:239
  2.2 0.0 copy-start.8
  2.2 1.0 %copy.19 = f16[4,8,8,1536]{3,2,0,1:T(8,128)(2,1)} copy(f16[4,8,8,1536]{3,2,1,0:T(8,128)(2,1)S(1)} %bitcast.28) | data formatting | bytes 1572864 | tf_op jit(solution)/shard_map/reshape | solution.py:239
  3.2 5.1 %all-to-all-start = ((f16[8,32,1536]{2,1,0:T(8,128)(2,1)}), f16[8,32,1536]{2,1,0:T(8,128)(2,1)S(1)}, u32[]{:S(2)}, u32[]{:S(2)}) async-start(f16[8,32,1536]{2,1,0:T(8,128)(2,1)} %bitcast.25), calls=%async_computation | async-start | bytes 1572864 | tf_op jit(solution)/shard_map/all_to_all | solution.py:240
  8.3 0.0 copy-done.8
  8.3 0.1 multiply_convert_fusion
  8.5 1.0 %copy.18 = f16[4,8,8,1536]{3,2,0,1:T(8,128)(2,1)} copy(f16[4,8,8,1536]{3,2,1,0:T(8,128)(2,1)S(1)} %bitcast.29) | data formatting | bytes 1572864 | tf_op jit(solution)/shard_map/reshape | solution.py:239
  9.5 11.0 %all-to-all-done = f16[8,32,1536]{2,1,0:T(8,128)(2,1)S(1)} async-done(((f16[8,32,1536]{2,1,0:T(8,128)(2,1)}), f16[8,32,1536]{2,1,0:T(8,128)(2,1)S(1)}, u32[]{:S(2)}, u32[]{:S(2)}) %all-to-all-start) | async-done | bytes 786464 | tf_op jit(solution)/shard_map/all_to_all | solution.py:240
  20.5 4.4 %all-to-all-start.1 = ((f16[8,32,1536]{2,1,0:T(8,128)(2,1)}), f16[8,32,1536]{2,1,0:T(8,128)(2,1)S(1)}, u32[]{:S(2)}, u32[]{:S(2)}) async-start(f16[8,32,1536]{2,1,0:T(8,128)(2,1)} %bitcast.23), calls=%async_computation.1 | async-start | bytes 1572864 | tf_op jit(solution)/shard_map/all_to_all | solution.py:240
  24.9 0.0 copy-start
  24.9 0.0 copy-start.1
  24.9 0.2 convert_multiply_fusion.1
  25.1 0.6 copy-done
  25.8 0.0 copy-done.1
  25.8 9.0 %compress.1 = (f32[64,1536]{1,0:T(8,128)}, bf16[384,256]{1,0:T(8,128)(2,1)S(1)}, f32[3,64,128]{2,1,0:T(8,128)}, bf16[192,256]{1,0:T(8,128)(2,1)S(1)}) custom-call(f32[256,1536]{1,0:T(8,128)S(1)} %bitcast.26, f32[64,256]{1,0:T(8,128)S(1)} %copy-done, f32[64,256]{1,0:T(8,128)S(1)} %copy-done.1), custom_call_target="tpu_custom_call" | custom-call | flops 12000000000 | bytes 12000000 | tf_op jit(solution)/shard_map/compress/pallas_call | solution.py:186
  34.8 0.0 copy-start.6
  34.8 0.0 copy-start.7
  34.8 2.3 %all-to-all-done.1 = f16[8,32,1536]{2,1,0:T(8,128)(2,1)S(1)} async-done(((f16[8,32,1536]{2,1,0:T(8,128)(2,1)}), f16[8,32,1536]{2,1,0:T(8,128)(2,1)S(1)}, u32[]{:S(2)}, u32[]{:S(2)}) %all-to-all-start.1) | async-done | bytes 786464 | tf_op jit(solution)/shard_map/all_to_all | solution.py:240
  37.1 0.2 convert_multiply_fusion
  37.3 0.0 copy-done.6
  37.3 0.0 copy-done.7
  37.3 0.0 copy-start.2
  37.3 0.0 copy-start.4
  37.4 1.3 %project.1 = (bf16[384,256]{1,0:T(8,128)(2,1)S(1)}, bf16[192,256]{1,0:T(8,128)(2,1)S(1)}) custom-call(f32[256,1536]{1,0:T(8,128)S(1)} %bitcast.27, f32[64,1536]{1,0:T(8,128)S(1)} %copy-done.6, f32[3,64,128]{2,1,0:T(8,128)S(1)} %copy-done.7), custom_call_target="tpu_custom_call" | custom-call | flops 4000000000 | bytes 4000000 | tf_op jit(solution)/shard_map/project/pallas_call | solution.py:206
  38.7 2.2 %collective-permute-start.3 = (bf16[192,256]{1,0:T(8,128)(2,1)S(1)}, bf16[192,256]{1,0:T(8,128)(2,1)S(1)}, u32[]{:S(2)}, u32[]{:S(2)}) collective-permute-start(bf16[192,256]{1,0:T(8,128)(2,1)S(1)} %get-tuple-element.15), channel_id=1, source_target_pairs={{8,16},{16,8},{24,32},{32,24},{40,48},{48,40},{56,64},{64,56},{72,... | collective-permute-start | bytes 294920 | tf_op jit(solution)/shard_map/ppermute | solution.py:282
  40.8 4.1 %collective-permute-start.2 = (bf16[192,256]{1,0:T(8,128)(2,1)S(1)}, bf16[192,256]{1,0:T(8,128)(2,1)S(1)}, u32[]{:S(2)}, u32[]{:S(2)}) collective-permute-start(bf16[192,256]{1,0:T(8,128)(2,1)S(1)} %get-tuple-element.15), channel_id=1, source_target_pairs={{0,8},{8,0},{16,24},{24,16},{32,40},{40,32},{48,56},{56,48},{64,72... | collective-permute-start | bytes 294920 | tf_op jit(solution)/shard_map/ppermute | solution.py:282
  45.0 3.6 %collective-permute-start.1 = (bf16[384,256]{1,0:T(8,128)(2,1)S(1)}, bf16[384,256]{1,0:T(8,128)(2,1)S(1)}, u32[]{:S(2)}, u32[]{:S(2)}) collective-permute-start(bf16[384,256]{1,0:T(8,128)(2,1)S(1)} %get-tuple-element.13.refs_0_), channel_id=1, source_target_pairs={{1,2},{2,1},{3,4},{4,3},{5,6},{6,5},{7,8},{8,7},{9,10},{10,9},{11,... | collective-permute-start | bytes 589832 | tf_op jit(solution)/shard_map/ppermute | solution.py:286
  48.6 2.5 %collective-permute-start = (bf16[384,256]{1,0:T(8,128)(2,1)S(1)}, bf16[384,256]{1,0:T(8,128)(2,1)S(1)}, u32[]{:S(2)}, u32[]{:S(2)}) collective-permute-start(bf16[384,256]{1,0:T(8,128)(2,1)S(1)} %get-tuple-element.13.refs_0_), channel_id=1, source_target_pairs={{0,1},{1,0},{2,3},{3,2},{4,5},{5,4},{6,7},{7,6},{8,9},{9,8},{10,11... | collective-permute-start | bytes 589832 | tf_op jit(solution)/shard_map/ppermute | solution.py:286
  51.1 0.0 collective-permute-done.2
  51.1 0.0 collective-permute-done.3
  51.2 1.3 %collective-permute-start.5 = (bf16[576,256]{1,0:T(8,128)(2,1)S(1)}, bf16[576,256]{1,0:T(8,128)(2,1)S(1)}, u32[]{:S(2)}, u32[]{:S(2)}) collective-permute-start(bf16[576,256]{1,0:T(8,128)(2,1)S(1)} %constant_dynamic-update-slice_fusion.refs_0_), channel_id=1, source_target_pairs={{24,48},{48,24},{72,96},{96,72},{120,144},{144,120},{168,192},{192... | collective-permute-start | bytes 884744 | tf_op jit(solution)/shard_map/ppermute | solution.py:288
  52.5 5.7 %collective-permute-start.4 = (bf16[576,256]{1,0:T(8,128)(2,1)S(1)}, bf16[576,256]{1,0:T(8,128)(2,1)S(1)}, u32[]{:S(2)}, u32[]{:S(2)}) collective-permute-start(bf16[576,256]{1,0:T(8,128)(2,1)S(1)} %constant_dynamic-update-slice_fusion.refs_0_), channel_id=1, source_target_pairs={{0,24},{24,0},{48,72},{72,48},{96,120},{120,96},{144,168},{168,144... | collective-permute-start | bytes 884744 | tf_op jit(solution)/shard_map/ppermute | solution.py:288
  58.2 0.0 collective-permute-done.1.refs_2_
  58.2 0.0 collective-permute-done.refs_1_
  58.2 0.0 copy-done.2
  58.2 0.0 copy-done.4
  58.2 0.0 copy-start.3
  58.2 0.0 copy-start.5
  58.2 2.3 %shard_map.111 = f32[1536,128]{1,0:T(8,128)} custom-call(s32[6,8]{1,0:T(8,128)S(1)} %copy-done.2, s32[6]{0:T(128)S(1)} %copy-done.4, bf16[384,256]{1,0:T(8,128)(2,1)S(1)} %get-tuple-element.11.left_ref, bf16[384,256]{1,0:T(8,128)(2,1)S(1)} %get-tuple-element.13.refs_0_, bf16[384,256]{1,0:T(8,128)(2,1)S(1)} %collective-permute-done.refs_1_, ...), custom_call_target="tpu_custom_call" | custom-call | flops 3000000000 | bytes 3000000 | tf_op jit(solution)/shard_map/pallas_call | solution.py:223
  60.5 11.3 %collective-permute-done.5.refs_2_ = bf16[576,256]{1,0:T(8,128)(2,1)S(1)} collective-permute-done((bf16[576,256]{1,0:T(8,128)(2,1)S(1)}, bf16[576,256]{1,0:T(8,128)(2,1)S(1)}, u32[]{:S(2)}, u32[]{:S(2)}) %collective-permute-start.5) | collective-permute-done | bytes 294944 | tf_op jit(solution)/shard_map/ppermute | solution.py:288
  71.9 0.0 collective-permute-done.4.refs_1_
  71.9 0.0 copy-done.3
  71.9 0.0 copy-done.5
  71.9 2.1 %shard_map.112 = f32[768,128]{1,0:T(8,128)} custom-call(s32[3,8]{1,0:T(4,128)S(1)} %copy-done.3, s32[3]{0:T(128)S(1)} %copy-done.5, bf16[192,256]{1,0:T(8,128)(2,1)S(1)} %get-tuple-element.14.left_ref, bf16[576,256]{1,0:T(8,128)(2,1)S(1)} %constant_dynamic-update-slice_fusion.refs_0_, bf16[576,256]{1,0:T(8,128)(2,1)S(1)} %collective-permute-done.4.refs_1_, ...), custom_call_target="tpu_custom_call" | custom-call | flops 3000000000 | bytes 3000000 | tf_op jit(solution)/shard_map/pallas_call | solution.py:223
  (3 shorter events, 0.0 us)
Async XLA Ops:
  2.2 6.2 %copy-start.8 = (f32[32,12288]{1,0:T(8,128)S(1)}, f32[32,12288]{1,0:T(8,128)}, u32[]{:S(2)}) copy-start(f32[32,12288]{1,0:T(8,128)} %param.9) | copy-start | bytes 4718596
  3.2 17.3 %all-to-all-start = ((f16[8,32,1536]{2,1,0:T(8,128)(2,1)}), f16[8,32,1536]{2,1,0:T(8,128)(2,1)S(1)}, u32[]{:S(2)}, u32[]{:S(2)}) async-start(f16[8,32,1536]{2,1,0:T(8,128)(2,1)} %bitcast.25), calls=%async_computation | async-start | bytes 1572864 | tf_op jit(solution)/shard_map/all_to_all | solution.py:240
  20.5 16.6 %all-to-all-start.1 = ((f16[8,32,1536]{2,1,0:T(8,128)(2,1)}), f16[8,32,1536]{2,1,0:T(8,128)(2,1)S(1)}, u32[]{:S(2)}, u32[]{:S(2)}) async-start(f16[8,32,1536]{2,1,0:T(8,128)(2,1)} %bitcast.23), calls=%async_computation.1 | async-start | bytes 1572864 | tf_op jit(solution)/shard_map/all_to_all | solution.py:240
  24.9 0.8 %copy-start = (f32[64,256]{1,0:T(8,128)S(1)}, f32[64,256]{1,0:T(8,128)}, u32[]{:S(2)}) copy-start(f32[64,256]{1,0:T(8,128)} %test_ref.1) | copy-start | bytes 196612
  24.9 0.9 %copy-start.1 = (f32[64,256]{1,0:T(8,128)S(1)}, f32[64,256]{1,0:T(8,128)}, u32[]{:S(2)}) copy-start(f32[64,256]{1,0:T(8,128)} %ptest_ref.1) | copy-start | bytes 196612
  34.8 2.6 %copy-start.6 = (f32[64,1536]{1,0:T(8,128)S(1)}, f32[64,1536]{1,0:T(8,128)}, u32[]{:S(2)}) copy-start(f32[64,1536]{1,0:T(8,128)} %get-tuple-element.6.basis_ref) | copy-start | bytes 1179652
  34.8 2.6 %copy-start.7 = (f32[3,64,128]{2,1,0:T(8,128)S(1)}, f32[3,64,128]{2,1,0:T(8,128)}, u32[]{:S(2)}) copy-start(f32[3,64,128]{2,1,0:T(8,128)} %get-tuple-element.8.transfer_ref) | copy-start | bytes 294916
  37.3 20.9 %copy-start.2 = (s32[6,8]{1,0:T(8,128)S(1)}, s32[6,8]{1,0:T(8,128)}, u32[]{:S(2)}) copy-start(s32[6,8]{1,0:T(8,128)} %far_ref.2) | copy-start | bytes 580
  37.3 20.9 %copy-start.4 = (s32[6]{0:T(128)S(1)}, s32[6]{0:T(128)}, u32[]{:S(2)}) copy-start(s32[6]{0:T(128)} %count_ref.2) | copy-start | bytes 76
  38.7 12.5 %collective-permute-start.3 = (bf16[192,256]{1,0:T(8,128)(2,1)S(1)}, bf16[192,256]{1,0:T(8,128)(2,1)S(1)}, u32[]{:S(2)}, u32[]{:S(2)}) collective-permute-start(bf16[192,256]{1,0:T(8,128)(2,1)S(1)} %get-tuple-element.15), channel_id=1, source_target_pairs={{8,16},{16,8},{24,32},{32,24},{40,48},{48,40},{56,64},{64,56},{72,... | collective-permute-start | bytes 294920 | tf_op jit(solution)/shard_map/ppermute | solution.py:282
  40.8 10.3 %collective-permute-start.2 = (bf16[192,256]{1,0:T(8,128)(2,1)S(1)}, bf16[192,256]{1,0:T(8,128)(2,1)S(1)}, u32[]{:S(2)}, u32[]{:S(2)}) collective-permute-start(bf16[192,256]{1,0:T(8,128)(2,1)S(1)} %get-tuple-element.15), channel_id=1, source_target_pairs={{0,8},{8,0},{16,24},{24,16},{32,40},{40,32},{48,56},{56,48},{64,72... | collective-permute-start | bytes 294920 | tf_op jit(solution)/shard_map/ppermute | solution.py:282
  45.0 13.2 %collective-permute-start.1 = (bf16[384,256]{1,0:T(8,128)(2,1)S(1)}, bf16[384,256]{1,0:T(8,128)(2,1)S(1)}, u32[]{:S(2)}, u32[]{:S(2)}) collective-permute-start(bf16[384,256]{1,0:T(8,128)(2,1)S(1)} %get-tuple-element.13.refs_0_), channel_id=1, source_target_pairs={{1,2},{2,1},{3,4},{4,3},{5,6},{6,5},{7,8},{8,7},{9,10},{10,9},{11,... | collective-permute-start | bytes 589832 | tf_op jit(solution)/shard_map/ppermute | solution.py:286
  48.6 9.6 %collective-permute-start = (bf16[384,256]{1,0:T(8,128)(2,1)S(1)}, bf16[384,256]{1,0:T(8,128)(2,1)S(1)}, u32[]{:S(2)}, u32[]{:S(2)}) collective-permute-start(bf16[384,256]{1,0:T(8,128)(2,1)S(1)} %get-tuple-element.13.refs_0_), channel_id=1, source_target_pairs={{0,1},{1,0},{2,3},{3,2},{4,5},{5,4},{6,7},{7,6},{8,9},{9,8},{10,11... | collective-permute-start | bytes 589832 | tf_op jit(solution)/shard_map/ppermute | solution.py:286
  51.2 20.7 %collective-permute-start.5 = (bf16[576,256]{1,0:T(8,128)(2,1)S(1)}, bf16[576,256]{1,0:T(8,128)(2,1)S(1)}, u32[]{:S(2)}, u32[]{:S(2)}) collective-permute-start(bf16[576,256]{1,0:T(8,128)(2,1)S(1)} %constant_dynamic-update-slice_fusion.refs_0_), channel_id=1, source_target_pairs={{24,48},{48,24},{72,96},{96,72},{120,144},{144,120},{168,192},{192... | collective-permute-start | bytes 884744 | tf_op jit(solution)/shard_map/ppermute | solution.py:288
  52.5 19.4 %collective-permute-start.4 = (bf16[576,256]{1,0:T(8,128)(2,1)S(1)}, bf16[576,256]{1,0:T(8,128)(2,1)S(1)}, u32[]{:S(2)}, u32[]{:S(2)}) collective-permute-start(bf16[576,256]{1,0:T(8,128)(2,1)S(1)} %constant_dynamic-update-slice_fusion.refs_0_), channel_id=1, source_target_pairs={{0,24},{24,0},{48,72},{72,48},{96,120},{120,96},{144,168},{168,144... | collective-permute-start | bytes 884744 | tf_op jit(solution)/shard_map/ppermute | solution.py:288
  58.2 13.6 %copy-start.3 = (s32[3,8]{1,0:T(4,128)S(1)}, s32[3,8]{1,0:T(4,128)}, u32[]{:S(2)}) copy-start(s32[3,8]{1,0:T(4,128)} %far_ref.3) | copy-start | bytes 292
  58.2 13.6 %copy-start.5 = (s32[3]{0:T(128)S(1)}, s32[3]{0:T(128)}, u32[]{:S(2)}) copy-start(s32[3]{0:T(128)} %count_ref.3) | copy-start | bytes 40

commit v3 on v2

--- a/solution.py
+++ b/solution.py
@@ -25,7 +25,18 @@
 def product(a, b, contract):
     dims = ((contract[0],), (contract[1],)), ((), ())
     dot = functools.partial(lax.dot_general, dimension_numbers=dims, preferred_element_type=f32)
-    return dot(a[0], b[0]) + (dot(a[1], b[0]) + dot(a[0], b[1]))
+    rows = a[0].shape[0]
+    both = dot(jnp.concatenate(a, axis=0), b[0])
+    return both[:rows] + (both[rows:] + dot(a[0], b[1]))
+
+
+def gram(a):
+    both = jnp.concatenate(a, axis=0)
+    rows = a[0].shape[0]
+    dims = (((1,), (1,)), ((), ()))
+    full = lax.dot_general(both, both, dims, preferred_element_type=f32)
+    total = full[:rows] + full[rows:]
+    return total[:, :rows] + total[:, rows:]
 
 
 def inverse_factors(packs):
@@ -95,19 +106,25 @@
             out_ref[start : start + RANK // 2, 128 * h : 128 * h + 128] = rows.astype(bf16)
 
 
-def compress(y_ref, test_ref, ptest_ref, basis_ref, w_ref, transfer_ref, a_ref, *halves):
+def prepare(*refs):
+    for ref, parts in zip(refs[:2], (refs[2:4], refs[4:])):
+        for part, value in zip(parts, split(ref[...])):
+            part[...] = value
+
+
+def compress(y_ref, test_high, test_low, ptest_high, ptest_low, basis_ref, w_ref, transfer_ref, a_ref, *halves):
     owned = y_ref.shape[1] // LEAF
     parents = owned // 2
-    test = split(test_ref[...])
+    test = test_high[...], test_low[...]
     ys, ks, grams = [], [], []
     for i in range(owned):
         y = split(y_ref[:, LEAF * i : LEAF * i + LEAF])
         ys.append(y)
         k = split(product(test, y, (1, 0)))
         ks.append(k)
-        grams.append(product(k, k, (1, 1)))
+        grams.append(gram(k))
     linvs = inverses(grams)
-    ptest = split(ptest_ref[...])
+    ptest = ptest_high[...], ptest_low[...]
     for i in range(owned):
         q = product(split(linvs[i]), ks[i], (1, 0))
         basis_ref[:, LEAF * i : LEAF * i + LEAF] = q
@@ -119,7 +136,7 @@
         stacks.append(stack)
         c = split(product(ptest, stack, (1, 1)))
         blocks.append(c)
-        grams.append(product(c, c, (1, 1)))
+        grams.append(gram(c))
     for i in range(owned):
         deinterleave(halves, i, w_ref)
     finvs = inverses(grams)
@@ -180,7 +197,45 @@
     return pl.CostEstimate(flops=us * 10**9, bytes_accessed=us * 10**6, transcendentals=0)
 
 
-def run_compress(y, test, ptest):
+def pack(x_ref, out_ref, sems):
+    parts, _, width = out_ref.shape
+    copies = [
+        pltpu.make_async_copy(x_ref.at[:, width * c : width * c + width], out_ref.at[c], sems.at[c])
+        for c in range(parts)
+    ]
+    for copy in copies:
+        copy.start()
+    for copy in copies:
+        copy.wait()
+
+
+def run_pack(x, parts):
+    rows, columns = x.shape
+    return pl.pallas_call(
+        pack,
+        out_shape=jax.ShapeDtypeStruct((parts, rows, columns // parts), f32),
+        in_specs=[pl.BlockSpec(memory_space=pltpu.HBM)],
+        out_specs=vmem,
+        scratch_shapes=[pltpu.SemaphoreType.DMA((parts,))],
+        compiler_params=params,
+        cost_estimate=cost(1),
+        name="pack",
+    )(pltpu.with_memory_space_constraint(x, pltpu.HBM))
+
+
+def run_prepare(test, ptest):
+    return pl.pallas_call(
+        prepare,
+        out_shape=[jax.ShapeDtypeStruct(x.shape, bf16) for x in (test, test, ptest, ptest)],
+        in_specs=[vmem] * 2,
+        out_specs=[vmem] * 4,
+        compiler_params=params,
+        cost_estimate=cost(1),
+        name="prepare",
+    )(test, ptest)
+
+
+def run_compress(y, tests):
     owned = y.shape[1] // LEAF
     samples = y.shape[0]
     return pl.pallas_call(
@@ -191,13 +246,13 @@
             jax.ShapeDtypeStruct((owned // 2, RANK, 2 * RANK), f32),
             jax.ShapeDtypeStruct((owned // 2 * RANK, samples), bf16),
         ),
-        in_specs=[vmem] * 3,
+        in_specs=[vmem] * 5,
         out_specs=(vmem,) * 4,
         scratch_shapes=[pltpu.VMEM((owned * RANK, 128), f32)] * (samples // 128),
         compiler_params=params,
         cost_estimate=cost(12),
         name="compress",
-    )(y, test, ptest)
+    )(y, *tests)
 
 
 def run_project(o, basis, transfer):
@@ -236,7 +291,7 @@
 def gathered(array):
     devices = lax.axis_size("samp")
     rows, columns = array.shape
-    sent = (array * SCALE).astype(jnp.float16).reshape(rows, devices, columns // devices).transpose(1, 0, 2)
+    sent = (run_pack(array, devices) * SCALE).astype(jnp.float16)
     got = lax.all_to_all(sent, "samp", split_axis=0, concat_axis=0, tiled=True)
     return got.astype(f32).reshape(rows * devices, columns // devices) * (1.0 / SCALE)
 
@@ -249,15 +304,13 @@
 
 
 def near_pairs(size):
-    return swaps(range(size), 0), swaps(range(size), 1)
+    return swaps(range(size), 1), swaps(range(size), 0)
 
 
 def far_pairs(rows):
-    sets = [[], []]
-    for start in range(3):
-        for late in range(2):
-            sets[late ^ (start == 1)] += swaps(range(start, rows, 3), late)
-    sets[1] += [(0, 2), (rows - 1, rows - 3)]
+    sets = [sum((swaps(range(start, rows, 3), late) for start in range(3)), []) for late in (1, 0)]
+    sets[0] += [(1, 2)]
+    sets[1] += [(rows - 2, rows - 3)]
     got = [{r} for r in range(rows)]
     for pairs in sets:
         assert len({i for i, _ in pairs}) == len({j for _, j in pairs}) == len(pairs)
@@ -276,7 +329,8 @@
     samp_count = lax.axis_size("samp")
     y = gathered(sketch)
     o = gathered(probes)
-    basis, w, transfer, a = run_compress(y, test_leaf, test_parent)
+    tests = run_prepare(test_leaf, test_parent)
+    basis, w, transfer, a = run_compress(y, tests)
     v, b = run_project(o, basis, transfer)
     pairs = near_pairs(row_count)
     near = [b] + [lax.ppermute(b, "rows", pairs[e]) for e in range(2)]
@@ -295,20 +349,18 @@
         def spot(leaf):
             later = (leaf >= first + owned).astype(jnp.int32)
             earlier = (leaf < first).astype(jnp.int32)
-            piece = later * (1 + odd) + earlier * (2 - odd)
+            piece = later * (2 - odd) + earlier * (1 + odd)
             return leaf - first + (earlier - later + piece) * owned
 
         return spot
 
     def parent_place():
         row = lax.axis_index("rows")
-        odd = lax.rem(row, 2)
-        start = lax.rem(row, 3)
-        behind = (lax.rem(lax.div(row, 3), 2) == 1) != (start == 1)
+        behind = lax.rem(lax.div(row, 3), 2) == 0
         one = jnp.where(behind, -(REACH - 1), REACH - 1)
         two = -one
-        two = jnp.where(row == 2, -2, two)
-        two = jnp.where(row == row_count - 3, 2, two)
+        one = jnp.where(row == 2, -1, one)
+        two = jnp.where(row == row_count - 3, 1, two)
         across = per_device * samp_count
 
         def spot(parent):
@@ -316,7 +368,7 @@
 
             def among(there, centre):
                 odd_there = lax.rem(row + centre + 2 * REACH, 2)
-                return jnp.where(there == 0, 0, jnp.where((there == 1) == (odd_there == 0), 1, 2))
+                return jnp.where(there == 0, 0, jnp.where((there == 1) == (odd_there == 1), 1, 2))
 
             far_at = jnp.where(abs(away - one) <= 1, 3 + among(away - one, one), 6 + among(away - two, two))
             at = jnp.where(abs(away) <= 1, among(away, 0), far_at)

time: 74.4 us -> 73.3 us (0.985)
  local copies, waits for them, and re-layouts: 2.76 us -> 0.06 us
  Pallas kernels: 14.6 us -> 16.9 us
  starting transfers between devices: 28.9 us -> 27 us
  waiting for transfers between devices: 24.7 us -> 25.7 us
    ppermute x2, starting transfers between devices: 7 us -> 3.21 us  [body(): far = [lax.ppermute(near, 'rows', pairs[e]) for e in range(2)]]
    pallas_call x0 -> x3, Pallas kernels: none -> 3.1 us  [the longest x2 3.08 us: run_pack(): pl.pallas_call(pack, out_shape=jax.ShapeDtypeStruct((parts, rows, columns...]
    ppermute x2, starting transfers between devices: 6.29 us -> 8.68 us  [body(): near = [b] + [lax.ppermute(b, 'rows', pairs[e]) for e in range(2)]]
    reshape x2 -> x0, local copies, waits for them, and re-layouts: 2.03 us -> none  [gathered(): (array * SCALE).astype(jnp.float16)]
    ppermute x2, waiting for transfers between devices: 0.01 us -> 1.87 us  [body(): halo = [v] + [lax.ppermute(v, both, pairs[e]) for e in range(2)]]
  transfers between devices with their start and end apart: 8 -> 8, of which waited for: 3 -> 5; matrix products, arithmetic and copies ran while one was open for 2% -> 2% of each run, Pallas kernels for 15% -> 17%
where the time goes in v3:
time: 73.3 us; the launch traced here: 72.9 us
  starting transfers between devices  27 us (37%)
  waiting for transfers between devices  25.7 us (35%)
  Pallas kernels  16.9 us (23%)
  other arithmetic  2.43 us (3%)
  between operations  0.84 us (1%)
    all_to_all x2, waiting for transfers between devices, gathered(): got = lax.all_to_all(sent, 'samp', split_axis=0, concat_axis=0, tiled=True)  13.2 us
    ppermute x2, waiting for transfers between devices, body(): far = [lax.ppermute(near, 'rows', pairs[e]) for e in range(2)]  10.7 us
    all_to_all x2, starting transfers between devices, gathered(): got = lax.all_to_all(sent, 'samp', split_axis=0, concat_axis=0, tiled=True)  9.56 us
    ppermute x2, starting transfers between devices, body(): near = [b] + [lax.ppermute(b, 'rows', pairs[e]) for e in range(2)]  8.68 us
    pallas_call x1, Pallas kernels, run_compress(): pl.pallas_call(compress, out_shape=(jax.ShapeDtypeStruct((RANK, y.shape[1...  8.32 us
    ppermute x2, starting transfers between devices, body(): halo = [v] + [lax.ppermute(v, both, pairs[e]) for e in range(2)]  5.54 us
    pallas_call x2, Pallas kernels, run_couple(): pl.pallas_call(functools.partial(couple, place), out_shape=jax.ShapeDtype...  4.33 us
    ppermute x2, starting transfers between devices, body(): far = [lax.ppermute(near, 'rows', pairs[e]) for e in range(2)]  3.21 us
  transfers between devices with their start and end apart: 8, of which 5 were waited for; matrix products, arithmetic and copies ran while one was open for 2% of the time, Pallas kernels for 17%

profile of v3, /device:TPU:5, one launch (start us, length us, event | category | flops | bytes accessed | tf_op | source)
XLA Modules:
  0.0 72.9 jit_solution(15510303702497625395)
XLA Ops:
  0.6 1.5 %pack.2 = f32[8,32,1536]{2,1,0:T(8,128)S(1)} custom-call(f32[32,12288]{1,0:T(8,128)} %x_ref.2), custom_call_target="tpu_custom_call" | custom-call | flops 1000000000 | bytes 1000000 | tf_op jit(solution)/shard_map/pack/pallas_call | solution.py:214
  2.2 1.0 %multiply_convert_fusion.1 = f16[8,32,1536]{2,1,0:T(8,128)(2,1)} fusion(f32[8,32,1536]{2,1,0:T(8,128)S(1)} %pack.2), kind=kLoop, calls=%fused_computation.3 | loop fusion | flops 786432 | bytes 2359296 | tf_op jit(solution)/shard_map/convert_element_type | solution.py:294
  3.2 5.1 %all-to-all-start = ((f16[8,32,1536]{2,1,0:T(8,128)(2,1)}), f16[8,32,1536]{2,1,0:T(8,128)(2,1)S(1)}, u32[]{:S(2)}, u32[]{:S(2)}) async-start(f16[8,32,1536]{2,1,0:T(8,128)(2,1)} %multiply_convert_fusion.1), calls=%async_computation | async-start | bytes 1572864 | tf_op jit(solution)/shard_map/all_to_all | solution.py:295
  8.3 0.0 copy-start
  8.3 0.0 copy-start.1
  8.3 1.6 %pack.3 = f32[8,32,1536]{2,1,0:T(8,128)S(1)} custom-call(f32[32,12288]{1,0:T(8,128)} %x_ref.3), custom_call_target="tpu_custom_call" | custom-call | flops 1000000000 | bytes 1000000 | tf_op jit(solution)/shard_map/pack/pallas_call | solution.py:214
  9.9 0.0 copy-done
  9.9 0.0 copy-done.1
  9.9 1.0 %multiply_convert_fusion = f16[8,32,1536]{2,1,0:T(8,128)(2,1)} fusion(f32[8,32,1536]{2,1,0:T(8,128)S(1)} %pack.3), kind=kLoop, calls=%fused_computation.1 | loop fusion | flops 786432 | bytes 2359296 | tf_op jit(solution)/shard_map/convert_element_type | solution.py:294
  10.9 9.5 %all-to-all-done = f16[8,32,1536]{2,1,0:T(8,128)(2,1)S(1)} async-done(((f16[8,32,1536]{2,1,0:T(8,128)(2,1)}), f16[8,32,1536]{2,1,0:T(8,128)(2,1)S(1)}, u32[]{:S(2)}, u32[]{:S(2)}) %all-to-all-start) | async-done | bytes 786464 | tf_op jit(solution)/shard_map/all_to_all | solution.py:295
  20.5 4.4 %all-to-all-start.1 = ((f16[8,32,1536]{2,1,0:T(8,128)(2,1)}), f16[8,32,1536]{2,1,0:T(8,128)(2,1)S(1)}, u32[]{:S(2)}, u32[]{:S(2)}) async-start(f16[8,32,1536]{2,1,0:T(8,128)(2,1)} %multiply_convert_fusion), calls=%async_computation.1 | async-start | bytes 1572864 | tf_op jit(solution)/shard_map/all_to_all | solution.py:295
  24.9 0.2 convert_multiply_fusion.1
  25.1 8.3 %compress.1 = (f32[64,1536]{1,0:T(8,128)}, bf16[384,256]{1,0:T(8,128)(2,1)S(1)}, f32[3,64,128]{2,1,0:T(8,128)}, bf16[192,256]{1,0:T(8,128)(2,1)S(1)}) custom-call(f32[256,1536]{1,0:T(8,128)S(1)} %bitcast.12, bf16[64,256]{1,0:T(8,128)(2,1)S(1)} %get-tuple-element.14.test_high, bf16[64,256]{1,0:T(8,128)(2,1)S(1)} %get-tuple-element.15.test_low, ...), custom_call_target="tpu_custom_call" | custom-call | flops 12000000000 | bytes 12000000 | tf_op jit(solution)/shard_map/compress/pallas_call | solution.py:241
  33.4 0.0 copy-start.6
  33.4 0.0 copy-start.7
  33.4 3.7 %all-to-all-done.1 = f16[8,32,1536]{2,1,0:T(8,128)(2,1)S(1)} async-done(((f16[8,32,1536]{2,1,0:T(8,128)(2,1)}), f16[8,32,1536]{2,1,0:T(8,128)(2,1)S(1)}, u32[]{:S(2)}, u32[]{:S(2)}) %all-to-all-start.1) | async-done | bytes 786464 | tf_op jit(solution)/shard_map/all_to_all | solution.py:295
  37.1 0.2 convert_multiply_fusion
  37.3 0.0 copy-done.6
  37.3 0.0 copy-done.7
  37.3 0.0 copy-start.2
  37.3 0.0 copy-start.4
  37.3 1.1 %project.1 = (bf16[384,256]{1,0:T(8,128)(2,1)S(1)}, bf16[192,256]{1,0:T(8,128)(2,1)S(1)}) custom-call(f32[256,1536]{1,0:T(8,128)S(1)} %bitcast.13, f32[64,1536]{1,0:T(8,128)S(1)} %copy-done.6, f32[3,64,128]{2,1,0:T(8,128)S(1)} %copy-done.7), custom_call_target="tpu_custom_call" | custom-call | flops 4000000000 | bytes 4000000 | tf_op jit(solution)/shard_map/project/pallas_call | solution.py:261
  38.5 2.8 %collective-permute-start.3 = (bf16[192,256]{1,0:T(8,128)(2,1)S(1)}, bf16[192,256]{1,0:T(8,128)(2,1)S(1)}, u32[]{:S(2)}, u32[]{:S(2)}) collective-permute-start(bf16[192,256]{1,0:T(8,128)(2,1)S(1)} %get-tuple-element.23), channel_id=1, source_target_pairs={{0,8},{8,0},{16,24},{24,16},{32,40},{40,32},{48,56},{56,48},{64,72... | collective-permute-start | bytes 294920 | tf_op jit(solution)/shard_map/ppermute | solution.py:336
  41.3 5.9 %collective-permute-start.2 = (bf16[192,256]{1,0:T(8,128)(2,1)S(1)}, bf16[192,256]{1,0:T(8,128)(2,1)S(1)}, u32[]{:S(2)}, u32[]{:S(2)}) collective-permute-start(bf16[192,256]{1,0:T(8,128)(2,1)S(1)} %get-tuple-element.23), channel_id=1, source_target_pairs={{8,16},{16,8},{24,32},{32,24},{40,48},{48,40},{56,64},{64,56},{72,... | collective-permute-start | bytes 294920 | tf_op jit(solution)/shard_map/ppermute | solution.py:336
  47.2 3.4 %collective-permute-start.1 = (bf16[384,256]{1,0:T(8,128)(2,1)S(1)}, bf16[384,256]{1,0:T(8,128)(2,1)S(1)}, u32[]{:S(2)}, u32[]{:S(2)}) collective-permute-start(bf16[384,256]{1,0:T(8,128)(2,1)S(1)} %get-tuple-element.21.refs_0_), channel_id=1, source_target_pairs={{0,1},{1,0},{2,3},{3,2},{4,5},{5,4},{6,7},{7,6},{8,9},{9,8},{10,11... | collective-permute-start | bytes 589832 | tf_op jit(solution)/shard_map/ppermute | solution.py:340
  50.6 2.1 %collective-permute-start = (bf16[384,256]{1,0:T(8,128)(2,1)S(1)}, bf16[384,256]{1,0:T(8,128)(2,1)S(1)}, u32[]{:S(2)}, u32[]{:S(2)}) collective-permute-start(bf16[384,256]{1,0:T(8,128)(2,1)S(1)} %get-tuple-element.21.refs_0_), channel_id=1, source_target_pairs={{1,2},{2,1},{3,4},{4,3},{5,6},{6,5},{7,8},{8,7},{9,10},{10,9},{11,... | collective-permute-start | bytes 589832 | tf_op jit(solution)/shard_map/ppermute | solution.py:340
  52.7 0.0 collective-permute-done.2
  52.7 0.0 collective-permute-done.3
  52.8 1.9 %collective-permute-start.5 = (bf16[576,256]{1,0:T(8,128)(2,1)S(1)}, bf16[576,256]{1,0:T(8,128)(2,1)S(1)}, u32[]{:S(2)}, u32[]{:S(2)}) collective-permute-start(bf16[576,256]{1,0:T(8,128)(2,1)S(1)} %constant_dynamic-update-slice_fusion.refs_0_), channel_id=1, source_target_pairs={{0,24},{24,0},{48,72},{72,48},{96,120},{120,96},{144,168},{168,144... | collective-permute-start | bytes 884744 | tf_op jit(solution)/shard_map/ppermute | solution.py:342
  54.7 1.3 %collective-permute-start.4 = (bf16[576,256]{1,0:T(8,128)(2,1)S(1)}, bf16[576,256]{1,0:T(8,128)(2,1)S(1)}, u32[]{:S(2)}, u32[]{:S(2)}) collective-permute-start(bf16[576,256]{1,0:T(8,128)(2,1)S(1)} %constant_dynamic-update-slice_fusion.refs_0_), channel_id=1, source_target_pairs={{24,48},{48,24},{72,96},{96,72},{120,144},{144,120},{168,192},{192... | collective-permute-start | bytes 884744 | tf_op jit(solution)/shard_map/ppermute | solution.py:342
  56.0 0.0 collective-permute-done.1.refs_2_
  56.0 1.9 %collective-permute-done.refs_1_ = bf16[384,256]{1,0:T(8,128)(2,1)S(1)} collective-permute-done((bf16[384,256]{1,0:T(8,128)(2,1)S(1)}, bf16[384,256]{1,0:T(8,128)(2,1)S(1)}, u32[]{:S(2)}, u32[]{:S(2)}) %collective-permute-start) | collective-permute-done | bytes 196640 | tf_op jit(solution)/shard_map/ppermute | solution.py:340
  57.9 0.0 copy-done.2
  57.9 0.0 copy-done.4
  57.9 0.0 copy-start.3
  57.9 0.0 copy-start.5
  57.9 2.3 %shard_map.111 = f32[1536,128]{1,0:T(8,128)} custom-call(s32[6,8]{1,0:T(8,128)S(1)} %copy-done.2, s32[6]{0:T(128)S(1)} %copy-done.4, bf16[384,256]{1,0:T(8,128)(2,1)S(1)} %get-tuple-element.19.left_ref, bf16[384,256]{1,0:T(8,128)(2,1)S(1)} %get-tuple-element.21.refs_0_, bf16[384,256]{1,0:T(8,128)(2,1)S(1)} %collective-permute-done.refs_1_, ...), custom_call_target="tpu_custom_call" | custom-call | flops 3000000000 | bytes 3000000 | tf_op jit(solution)/shard_map/pallas_call | solution.py:278
  60.2 3.5 %collective-permute-done.5.refs_2_ = bf16[576,256]{1,0:T(8,128)(2,1)S(1)} collective-permute-done((bf16[576,256]{1,0:T(8,128)(2,1)S(1)}, bf16[576,256]{1,0:T(8,128)(2,1)S(1)}, u32[]{:S(2)}, u32[]{:S(2)}) %collective-permute-start.5) | collective-permute-done | bytes 294944 | tf_op jit(solution)/shard_map/ppermute | solution.py:342
  63.7 7.2 %collective-permute-done.4.refs_1_ = bf16[576,256]{1,0:T(8,128)(2,1)S(1)} collective-permute-done((bf16[576,256]{1,0:T(8,128)(2,1)S(1)}, bf16[576,256]{1,0:T(8,128)(2,1)S(1)}, u32[]{:S(2)}, u32[]{:S(2)}) %collective-permute-start.4) | collective-permute-done | bytes 294944 | tf_op jit(solution)/shard_map/ppermute | solution.py:342
  70.8 0.0 copy-done.3
  70.8 0.0 copy-done.5
  70.8 2.1 %shard_map.112 = f32[768,128]{1,0:T(8,128)} custom-call(s32[3,8]{1,0:T(4,128)S(1)} %copy-done.3, s32[3]{0:T(128)S(1)} %copy-done.5, bf16[192,256]{1,0:T(8,128)(2,1)S(1)} %get-tuple-element.22.left_ref, bf16[576,256]{1,0:T(8,128)(2,1)S(1)} %constant_dynamic-update-slice_fusion.refs_0_, bf16[576,256]{1,0:T(8,128)(2,1)S(1)} %collective-permute-done.4.refs_1_, ...), custom_call_target="tpu_custom_call" | custom-call | flops 3000000000 | bytes 3000000 | tf_op jit(solution)/shard_map/pallas_call | solution.py:278
  (4 shorter events, 0.0 us)
Async XLA Ops:
  3.2 17.3 %all-to-all-start = ((f16[8,32,1536]{2,1,0:T(8,128)(2,1)}), f16[8,32,1536]{2,1,0:T(8,128)(2,1)S(1)}, u32[]{:S(2)}, u32[]{:S(2)}) async-start(f16[8,32,1536]{2,1,0:T(8,128)(2,1)} %multiply_convert_fusion.1), calls=%async_computation | async-start | bytes 1572864 | tf_op jit(solution)/shard_map/all_to_all | solution.py:295
  8.3 1.6 %copy-start = (f32[64,256]{1,0:T(8,128)S(1)}, f32[64,256]{1,0:T(8,128)}, u32[]{:S(2)}) copy-start(f32[64,256]{1,0:T(8,128)} %refs_0_.1) | copy-start | bytes 196612
  8.3 1.6 %copy-start.1 = (f32[64,256]{1,0:T(8,128)S(1)}, f32[64,256]{1,0:T(8,128)}, u32[]{:S(2)}) copy-start(f32[64,256]{1,0:T(8,128)} %refs_1_.1) | copy-start | bytes 196612
  20.5 16.6 %all-to-all-start.1 = ((f16[8,32,1536]{2,1,0:T(8,128)(2,1)}), f16[8,32,1536]{2,1,0:T(8,128)(2,1)S(1)}, u32[]{:S(2)}, u32[]{:S(2)}) async-start(f16[8,32,1536]{2,1,0:T(8,128)(2,1)} %multiply_convert_fusion), calls=%async_computation.1 | async-start | bytes 1572864 | tf_op jit(solution)/shard_map/all_to_all | solution.py:295
  33.4 3.9 %copy-start.6 = (f32[64,1536]{1,0:T(8,128)S(1)}, f32[64,1536]{1,0:T(8,128)}, u32[]{:S(2)}) copy-start(f32[64,1536]{1,0:T(8,128)} %get-tuple-element.10.basis_ref) | copy-start | bytes 1179652
  33.4 3.9 %copy-start.7 = (f32[3,64,128]{2,1,0:T(8,128)S(1)}, f32[3,64,128]{2,1,0:T(8,128)}, u32[]{:S(2)}) copy-start(f32[3,64,128]{2,1,0:T(8,128)} %get-tuple-element.12.transfer_ref) | copy-start | bytes 294916
  37.3 20.6 %copy-start.2 = (s32[6,8]{1,0:T(8,128)S(1)}, s32[6,8]{1,0:T(8,128)}, u32[]{:S(2)}) copy-start(s32[6,8]{1,0:T(8,128)} %far_ref.2) | copy-start | bytes 580
  37.3 20.6 %copy-start.4 = (s32[6]{0:T(128)S(1)}, s32[6]{0:T(128)}, u32[]{:S(2)}) copy-start(s32[6]{0:T(128)} %count_ref.2) | copy-start | bytes 76
  38.5 14.3 %collective-permute-start.3 = (bf16[192,256]{1,0:T(8,128)(2,1)S(1)}, bf16[192,256]{1,0:T(8,128)(2,1)S(1)}, u32[]{:S(2)}, u32[]{:S(2)}) collective-permute-start(bf16[192,256]{1,0:T(8,128)(2,1)S(1)} %get-tuple-element.23), channel_id=1, source_target_pairs={{0,8},{8,0},{16,24},{24,16},{32,40},{40,32},{48,56},{56,48},{64,72... | collective-permute-start | bytes 294920 | tf_op jit(solution)/shard_map/ppermute | solution.py:336
  41.3 11.4 %collective-permute-start.2 = (bf16[192,256]{1,0:T(8,128)(2,1)S(1)}, bf16[192,256]{1,0:T(8,128)(2,1)S(1)}, u32[]{:S(2)}, u32[]{:S(2)}) collective-permute-start(bf16[192,256]{1,0:T(8,128)(2,1)S(1)} %get-tuple-element.23), channel_id=1, source_target_pairs={{8,16},{16,8},{24,32},{32,24},{40,48},{48,40},{56,64},{64,56},{72,... | collective-permute-start | bytes 294920 | tf_op jit(solution)/shard_map/ppermute | solution.py:336
  47.2 8.9 %collective-permute-start.1 = (bf16[384,256]{1,0:T(8,128)(2,1)S(1)}, bf16[384,256]{1,0:T(8,128)(2,1)S(1)}, u32[]{:S(2)}, u32[]{:S(2)}) collective-permute-start(bf16[384,256]{1,0:T(8,128)(2,1)S(1)} %get-tuple-element.21.refs_0_), channel_id=1, source_target_pairs={{0,1},{1,0},{2,3},{3,2},{4,5},{5,4},{6,7},{7,6},{8,9},{9,8},{10,11... | collective-permute-start | bytes 589832 | tf_op jit(solution)/shard_map/ppermute | solution.py:340
  50.6 7.3 %collective-permute-start = (bf16[384,256]{1,0:T(8,128)(2,1)S(1)}, bf16[384,256]{1,0:T(8,128)(2,1)S(1)}, u32[]{:S(2)}, u32[]{:S(2)}) collective-permute-start(bf16[384,256]{1,0:T(8,128)(2,1)S(1)} %get-tuple-element.21.refs_0_), channel_id=1, source_target_pairs={{1,2},{2,1},{3,4},{4,3},{5,6},{6,5},{7,8},{8,7},{9,10},{10,9},{11,... | collective-permute-start | bytes 589832 | tf_op jit(solution)/shard_map/ppermute | solution.py:340
  52.8 10.9 %collective-permute-start.5 = (bf16[576,256]{1,0:T(8,128)(2,1)S(1)}, bf16[576,256]{1,0:T(8,128)(2,1)S(1)}, u32[]{:S(2)}, u32[]{:S(2)}) collective-permute-start(bf16[576,256]{1,0:T(8,128)(2,1)S(1)} %constant_dynamic-update-slice_fusion.refs_0_), channel_id=1, source_target_pairs={{0,24},{24,0},{48,72},{72,48},{96,120},{120,96},{144,168},{168,144... | collective-permute-start | bytes 884744 | tf_op jit(solution)/shard_map/ppermute | solution.py:342
  54.7 16.1 %collective-permute-start.4 = (bf16[576,256]{1,0:T(8,128)(2,1)S(1)}, bf16[576,256]{1,0:T(8,128)(2,1)S(1)}, u32[]{:S(2)}, u32[]{:S(2)}) collective-permute-start(bf16[576,256]{1,0:T(8,128)(2,1)S(1)} %constant_dynamic-update-slice_fusion.refs_0_), channel_id=1, source_target_pairs={{24,48},{48,24},{72,96},{96,72},{120,144},{144,120},{168,192},{192... | collective-permute-start | bytes 884744 | tf_op jit(solution)/shard_map/ppermute | solution.py:342
  57.9 12.9 %copy-start.3 = (s32[3,8]{1,0:T(4,128)S(1)}, s32[3,8]{1,0:T(4,128)}, u32[]{:S(2)}) copy-start(s32[3,8]{1,0:T(4,128)} %far_ref.3) | copy-start | bytes 292
  57.9 12.9 %copy-start.5 = (s32[3]{0:T(128)S(1)}, s32[3]{0:T(128)}, u32[]{:S(2)}) copy-start(s32[3]{0:T(128)} %count_ref.3) | copy-start | bytes 40

commit v4 on v3

--- a/solution.py
+++ b/solution.py
@@ -161,7 +161,7 @@
 
 
 def couple(place, far_ref, count_ref, left_ref, *refs):
-    pieces, out_ref, table = refs[:-2], refs[-2], refs[-1]
+    pieces, (out_ref, table, stage, sems) = refs[:-4], refs[-4:]
     rows = left_ref.shape[0] // RANK
     slots = far_ref.shape[1]
     at = 0
@@ -175,6 +175,7 @@
     samples = left_ref.shape[1]
     dims = (((1,), (1,)), ((), ()))
     spot = place()
+    copies = []
     for i in range(rows):
         left = left_ref[RANK * i : RANK * i + RANK, :]
         for k in range(0, slots, 2):
@@ -185,7 +186,12 @@
             second = jnp.where(low, pltpu.roll(even, RANK, 1), odd)
             for e, value in enumerate((first, second)):
                 scale = jnp.where(k + e < count_ref[i], 1.0 / samples, 0.0).astype(f32)
-                out_ref[pl.ds(i * 4 * RANK + k + e, RANK // 2, stride=8), :] = value * scale
+                stage[pl.ds(i * 4 * RANK + k + e, RANK // 2, stride=8), :] = value * scale
+        done = pl.ds(i * 4 * RANK, 4 * RANK)
+        copies.append(pltpu.make_async_copy(stage.at[done, :], out_ref.at[done, :], sems.at[i]))
+        copies[i].start()
+    for copy in copies:
+        copy.wait()
 
 
 vmem = pl.BlockSpec(memory_space=pltpu.VMEM)
@@ -279,8 +285,12 @@
         functools.partial(couple, place),
         out_shape=jax.ShapeDtypeStruct((rows * 4 * RANK, 128), f32),
         in_specs=[smem, smem, vmem] + [vmem] * len(pieces),
-        out_specs=vmem,
-        scratch_shapes=[pltpu.VMEM((total, RANK, left.shape[1]), bf16)],
+        out_specs=pl.BlockSpec(memory_space=pl.ANY),
+        scratch_shapes=[
+            pltpu.VMEM((total, RANK, left.shape[1]), bf16),
+            pltpu.VMEM((rows * 4 * RANK, 128), f32),
+            pltpu.SemaphoreType.DMA((rows,)),
+        ],
         compiler_params=params,
         cost_estimate=cost(3),
     )(far, count, left, *pieces)
@@ -308,9 +318,11 @@
 
 
 def far_pairs(rows):
-    sets = [sum((swaps(range(start, rows, 3), late) for start in range(3)), []) for late in (1, 0)]
-    sets[0] += [(1, 2)]
-    sets[1] += [(rows - 2, rows - 3)]
+    sets = [[], []]
+    for start in range(3):
+        for late in range(2):
+            sets[late ^ (start != 1)] += swaps(range(start, rows, 3), late)
+    sets[0] += [(0, 2), (rows - 1, rows - 3)]
     got = [{r} for r in range(rows)]
     for pairs in sets:
         assert len({i for i, _ in pairs}) == len({j for _, j in pairs}) == len(pairs)
@@ -356,11 +368,11 @@
 
     def parent_place():
         row = lax.axis_index("rows")
-        behind = lax.rem(lax.div(row, 3), 2) == 0
+        behind = (lax.rem(lax.div(row, 3), 2) == 0) != (lax.rem(row, 3) == 1)
         one = jnp.where(behind, -(REACH - 1), REACH - 1)
         two = -one
-        one = jnp.where(row == 2, -1, one)
-        two = jnp.where(row == row_count - 3, 1, two)
+        one = jnp.where(row == 2, -2, one)
+        one = jnp.where(row == row_count - 3, 2, one)
         across = per_device * samp_count
 
         def spot(parent):

time: 73.3 us -> 74.8 us (1.020)
  waiting for transfers between devices: 25.7 us -> 27.4 us
    ppermute x2, waiting for transfers between devices: 10.7 us -> 12.3 us  [body(): far = [lax.ppermute(near, 'rows', pairs[e]) for e in range(2)]]
  transfers between devices with their start and end apart: 8 -> 8, of which waited for: 5 -> 5; matrix products, arithmetic and copies ran while one was open for 2% -> 2% of each run, Pallas kernels for 17% -> 16%
where the time goes in v4:
time: 74.8 us; the launch traced here: 74.3 us
  waiting for transfers between devices  27.4 us (37%)
  starting transfers between devices  27 us (36%)
  Pallas kernels  16.6 us (22%)
  other arithmetic  2.43 us (3%)
  between operations  0.84 us (1%)
    all_to_all x2, waiting for transfers between devices, gathered(): got = lax.all_to_all(sent, 'samp', split_axis=0, concat_axis=0, tiled=True)  13.2 us
    ppermute x2, waiting for transfers between devices, body(): far = [lax.ppermute(near, 'rows', pairs[e]) for e in range(2)]  12.3 us
    all_to_all x2, starting transfers between devices, gathered(): got = lax.all_to_all(sent, 'samp', split_axis=0, concat_axis=0, tiled=True)  9.56 us
    ppermute x2, starting transfers between devices, body(): near = [b] + [lax.ppermute(b, 'rows', pairs[e]) for e in range(2)]  8.68 us
    pallas_call x1, Pallas kernels, run_compress(): pl.pallas_call(compress, out_shape=(jax.ShapeDtypeStruct((RANK, y.shape[1...  8.32 us
    ppermute x2, starting transfers between devices, body(): halo = [v] + [lax.ppermute(v, both, pairs[e]) for e in range(2)]  5.54 us
    pallas_call x2, Pallas kernels, run_couple(): pl.pallas_call(functools.partial(couple, place), out_shape=jax.ShapeDtype...  4.09 us
    ppermute x2, starting transfers between devices, body(): far = [lax.ppermute(near, 'rows', pairs[e]) for e in range(2)]  3.21 us
  transfers between devices with their start and end apart: 8, of which 5 were waited for; matrix products, arithmetic and copies ran while one was open for 2% of the time, Pallas kernels for 16%

profile of v4, /device:TPU:5, one launch (start us, length us, event | category | flops | bytes accessed | tf_op | source)
XLA Modules:
  0.0 74.3 jit_solution(15187011935744539141)
XLA Ops:
  0.6 1.5 %pack.2 = f32[8,32,1536]{2,1,0:T(8,128)S(1)} custom-call(f32[32,12288]{1,0:T(8,128)} %x_ref.2), custom_call_target="tpu_custom_call" | custom-call | flops 1000000000 | bytes 1000000 | tf_op jit(solution)/shard_map/pack/pallas_call | solution.py:220
  2.2 1.0 %multiply_convert_fusion.1 = f16[8,32,1536]{2,1,0:T(8,128)(2,1)} fusion(f32[8,32,1536]{2,1,0:T(8,128)S(1)} %pack.2), kind=kLoop, calls=%fused_computation.3 | loop fusion | flops 786432 | bytes 2359296 | tf_op jit(solution)/shard_map/convert_element_type | solution.py:304
  3.2 5.1 %all-to-all-start = ((f16[8,32,1536]{2,1,0:T(8,128)(2,1)}), f16[8,32,1536]{2,1,0:T(8,128)(2,1)S(1)}, u32[]{:S(2)}, u32[]{:S(2)}) async-start(f16[8,32,1536]{2,1,0:T(8,128)(2,1)} %multiply_convert_fusion.1), calls=%async_computation | async-start | bytes 1572864 | tf_op jit(solution)/shard_map/all_to_all | solution.py:305
  8.3 0.0 copy-start
  8.3 0.0 copy-start.1
  8.3 1.6 %pack.3 = f32[8,32,1536]{2,1,0:T(8,128)S(1)} custom-call(f32[32,12288]{1,0:T(8,128)} %x_ref.3), custom_call_target="tpu_custom_call" | custom-call | flops 1000000000 | bytes 1000000 | tf_op jit(solution)/shard_map/pack/pallas_call | solution.py:220
  9.9 0.0 copy-done
  9.9 0.0 copy-done.1
  9.9 1.0 %multiply_convert_fusion = f16[8,32,1536]{2,1,0:T(8,128)(2,1)} fusion(f32[8,32,1536]{2,1,0:T(8,128)S(1)} %pack.3), kind=kLoop, calls=%fused_computation.1 | loop fusion | flops 786432 | bytes 2359296 | tf_op jit(solution)/shard_map/convert_element_type | solution.py:304
  10.9 9.5 %all-to-all-done = f16[8,32,1536]{2,1,0:T(8,128)(2,1)S(1)} async-done(((f16[8,32,1536]{2,1,0:T(8,128)(2,1)}), f16[8,32,1536]{2,1,0:T(8,128)(2,1)S(1)}, u32[]{:S(2)}, u32[]{:S(2)}) %all-to-all-start) | async-done | bytes 786464 | tf_op jit(solution)/shard_map/all_to_all | solution.py:305
  20.5 4.4 %all-to-all-start.1 = ((f16[8,32,1536]{2,1,0:T(8,128)(2,1)}), f16[8,32,1536]{2,1,0:T(8,128)(2,1)S(1)}, u32[]{:S(2)}, u32[]{:S(2)}) async-start(f16[8,32,1536]{2,1,0:T(8,128)(2,1)} %multiply_convert_fusion), calls=%async_computation.1 | async-start | bytes 1572864 | tf_op jit(solution)/shard_map/all_to_all | solution.py:305
  24.9 0.2 convert_multiply_fusion.1
  25.1 8.3 %compress.1 = (f32[64,1536]{1,0:T(8,128)}, bf16[384,256]{1,0:T(8,128)(2,1)S(1)}, f32[3,64,128]{2,1,0:T(8,128)}, bf16[192,256]{1,0:T(8,128)(2,1)S(1)}) custom-call(f32[256,1536]{1,0:T(8,128)S(1)} %bitcast.12, bf16[64,256]{1,0:T(8,128)(2,1)S(1)} %get-tuple-element.14.test_high, bf16[64,256]{1,0:T(8,128)(2,1)S(1)} %get-tuple-element.15.test_low, ...), custom_call_target="tpu_custom_call" | custom-call | flops 12000000000 | bytes 12000000 | tf_op jit(solution)/shard_map/compress/pallas_call | solution.py:247
  33.4 0.0 copy-start.6
  33.4 0.0 copy-start.7
  33.4 3.7 %all-to-all-done.1 = f16[8,32,1536]{2,1,0:T(8,128)(2,1)S(1)} async-done(((f16[8,32,1536]{2,1,0:T(8,128)(2,1)}), f16[8,32,1536]{2,1,0:T(8,128)(2,1)S(1)}, u32[]{:S(2)}, u32[]{:S(2)}) %all-to-all-start.1) | async-done | bytes 786464 | tf_op jit(solution)/shard_map/all_to_all | solution.py:305
  37.1 0.2 convert_multiply_fusion
  37.3 0.0 copy-done.6
  37.3 0.0 copy-done.7
  37.3 0.0 copy-start.2
  37.3 0.0 copy-start.4
  37.3 1.1 %project.1 = (bf16[384,256]{1,0:T(8,128)(2,1)S(1)}, bf16[192,256]{1,0:T(8,128)(2,1)S(1)}) custom-call(f32[256,1536]{1,0:T(8,128)S(1)} %bitcast.13, f32[64,1536]{1,0:T(8,128)S(1)} %copy-done.6, f32[3,64,128]{2,1,0:T(8,128)S(1)} %copy-done.7), custom_call_target="tpu_custom_call" | custom-call | flops 4000000000 | bytes 4000000 | tf_op jit(solution)/shard_map/project/pallas_call | solution.py:267
  38.5 2.8 %collective-permute-start.3 = (bf16[192,256]{1,0:T(8,128)(2,1)S(1)}, bf16[192,256]{1,0:T(8,128)(2,1)S(1)}, u32[]{:S(2)}, u32[]{:S(2)}) collective-permute-start(bf16[192,256]{1,0:T(8,128)(2,1)S(1)} %get-tuple-element.23), channel_id=1, source_target_pairs={{0,8},{8,0},{16,24},{24,16},{32,40},{40,32},{48,56},{56,48},{64,72... | collective-permute-start | bytes 294920 | tf_op jit(solution)/shard_map/ppermute | solution.py:348
  41.3 5.9 %collective-permute-start.2 = (bf16[192,256]{1,0:T(8,128)(2,1)S(1)}, bf16[192,256]{1,0:T(8,128)(2,1)S(1)}, u32[]{:S(2)}, u32[]{:S(2)}) collective-permute-start(bf16[192,256]{1,0:T(8,128)(2,1)S(1)} %get-tuple-element.23), channel_id=1, source_target_pairs={{8,16},{16,8},{24,32},{32,24},{40,48},{48,40},{56,64},{64,56},{72,... | collective-permute-start | bytes 294920 | tf_op jit(solution)/shard_map/ppermute | solution.py:348
  47.2 3.4 %collective-permute-start.1 = (bf16[384,256]{1,0:T(8,128)(2,1)S(1)}, bf16[384,256]{1,0:T(8,128)(2,1)S(1)}, u32[]{:S(2)}, u32[]{:S(2)}) collective-permute-start(bf16[384,256]{1,0:T(8,128)(2,1)S(1)} %get-tuple-element.21.refs_0_), channel_id=1, source_target_pairs={{0,1},{1,0},{2,3},{3,2},{4,5},{5,4},{6,7},{7,6},{8,9},{9,8},{10,11... | collective-permute-start | bytes 589832 | tf_op jit(solution)/shard_map/ppermute | solution.py:352
  50.6 2.1 %collective-permute-start = (bf16[384,256]{1,0:T(8,128)(2,1)S(1)}, bf16[384,256]{1,0:T(8,128)(2,1)S(1)}, u32[]{:S(2)}, u32[]{:S(2)}) collective-permute-start(bf16[384,256]{1,0:T(8,128)(2,1)S(1)} %get-tuple-element.21.refs_0_), channel_id=1, source_target_pairs={{1,2},{2,1},{3,4},{4,3},{5,6},{6,5},{7,8},{8,7},{9,10},{10,9},{11,... | collective-permute-start | bytes 589832 | tf_op jit(solution)/shard_map/ppermute | solution.py:352
  52.7 0.0 collective-permute-done.2
  52.7 0.0 collective-permute-done.3
  52.8 1.9 %collective-permute-start.5 = (bf16[576,256]{1,0:T(8,128)(2,1)S(1)}, bf16[576,256]{1,0:T(8,128)(2,1)S(1)}, u32[]{:S(2)}, u32[]{:S(2)}) collective-permute-start(bf16[576,256]{1,0:T(8,128)(2,1)S(1)} %constant_dynamic-update-slice_fusion.refs_0_), channel_id=1, source_target_pairs={{0,24},{24,0},{48,72},{72,48},{96,120},{120,96},{144,168},{168,144... | collective-permute-start | bytes 884744 | tf_op jit(solution)/shard_map/ppermute | solution.py:354
  54.7 1.3 %collective-permute-start.4 = (bf16[576,256]{1,0:T(8,128)(2,1)S(1)}, bf16[576,256]{1,0:T(8,128)(2,1)S(1)}, u32[]{:S(2)}, u32[]{:S(2)}) collective-permute-start(bf16[576,256]{1,0:T(8,128)(2,1)S(1)} %constant_dynamic-update-slice_fusion.refs_0_), channel_id=1, source_target_pairs={{24,48},{48,24},{72,96},{96,72},{120,144},{144,120},{168,192},{192... | collective-permute-start | bytes 884744 | tf_op jit(solution)/shard_map/ppermute | solution.py:354
  56.0 0.0 collective-permute-done.1.refs_2_
  56.0 1.9 %collective-permute-done.refs_1_ = bf16[384,256]{1,0:T(8,128)(2,1)S(1)} collective-permute-done((bf16[384,256]{1,0:T(8,128)(2,1)S(1)}, bf16[384,256]{1,0:T(8,128)(2,1)S(1)}, u32[]{:S(2)}, u32[]{:S(2)}) %collective-permute-start) | collective-permute-done | bytes 196640 | tf_op jit(solution)/shard_map/ppermute | solution.py:352
  57.9 0.0 copy-done.2
  57.9 0.0 copy-done.4
  57.9 0.0 copy-start.3
  57.9 0.0 copy-start.5
  57.9 2.1 %shard_map.111 = f32[1536,128]{1,0:T(8,128)} custom-call(s32[6,8]{1,0:T(8,128)S(1)} %copy-done.2, s32[6]{0:T(128)S(1)} %copy-done.4, bf16[384,256]{1,0:T(8,128)(2,1)S(1)} %get-tuple-element.19.left_ref, bf16[384,256]{1,0:T(8,128)(2,1)S(1)} %get-tuple-element.21.refs_0_, bf16[384,256]{1,0:T(8,128)(2,1)S(1)} %collective-permute-done.refs_1_, ...), custom_call_target="tpu_custom_call" | custom-call | flops 3000000000 | bytes 3000000 | tf_op jit(solution)/shard_map/pallas_call | solution.py:284
  60.0 3.7 %collective-permute-done.5.refs_2_ = bf16[576,256]{1,0:T(8,128)(2,1)S(1)} collective-permute-done((bf16[576,256]{1,0:T(8,128)(2,1)S(1)}, bf16[576,256]{1,0:T(8,128)(2,1)S(1)}, u32[]{:S(2)}, u32[]{:S(2)}) %collective-permute-start.5) | collective-permute-done | bytes 294944 | tf_op jit(solution)/shard_map/ppermute | solution.py:354
  63.7 8.7 %collective-permute-done.4.refs_1_ = bf16[576,256]{1,0:T(8,128)(2,1)S(1)} collective-permute-done((bf16[576,256]{1,0:T(8,128)(2,1)S(1)}, bf16[576,256]{1,0:T(8,128)(2,1)S(1)}, u32[]{:S(2)}, u32[]{:S(2)}) %collective-permute-start.4) | collective-permute-done | bytes 294944 | tf_op jit(solution)/shard_map/ppermute | solution.py:354
  72.3 0.0 copy-done.3
  72.3 0.0 copy-done.5
  72.3 2.0 %shard_map.112 = f32[768,128]{1,0:T(8,128)} custom-call(s32[3,8]{1,0:T(4,128)S(1)} %copy-done.3, s32[3]{0:T(128)S(1)} %copy-done.5, bf16[192,256]{1,0:T(8,128)(2,1)S(1)} %get-tuple-element.22.left_ref, bf16[576,256]{1,0:T(8,128)(2,1)S(1)} %constant_dynamic-update-slice_fusion.refs_0_, bf16[576,256]{1,0:T(8,128)(2,1)S(1)} %collective-permute-done.4.refs_1_, ...), custom_call_target="tpu_custom_call" | custom-call | flops 3000000000 | bytes 3000000 | tf_op jit(solution)/shard_map/pallas_call | solution.py:284
  (4 shorter events, 0.0 us)
Async XLA Ops:
  3.2 17.3 %all-to-all-start = ((f16[8,32,1536]{2,1,0:T(8,128)(2,1)}), f16[8,32,1536]{2,1,0:T(8,128)(2,1)S(1)}, u32[]{:S(2)}, u32[]{:S(2)}) async-start(f16[8,32,1536]{2,1,0:T(8,128)(2,1)} %multiply_convert_fusion.1), calls=%async_computation | async-start | bytes 1572864 | tf_op jit(solution)/shard_map/all_to_all | solution.py:305
  8.3 1.6 %copy-start = (f32[64,256]{1,0:T(8,128)S(1)}, f32[64,256]{1,0:T(8,128)}, u32[]{:S(2)}) copy-start(f32[64,256]{1,0:T(8,128)} %refs_0_.1) | copy-start | bytes 196612
  8.3 1.6 %copy-start.1 = (f32[64,256]{1,0:T(8,128)S(1)}, f32[64,256]{1,0:T(8,128)}, u32[]{:S(2)}) copy-start(f32[64,256]{1,0:T(8,128)} %refs_1_.1) | copy-start | bytes 196612
  20.5 16.6 %all-to-all-start.1 = ((f16[8,32,1536]{2,1,0:T(8,128)(2,1)}), f16[8,32,1536]{2,1,0:T(8,128)(2,1)S(1)}, u32[]{:S(2)}, u32[]{:S(2)}) async-start(f16[8,32,1536]{2,1,0:T(8,128)(2,1)} %multiply_convert_fusion), calls=%async_computation.1 | async-start | bytes 1572864 | tf_op jit(solution)/shard_map/all_to_all | solution.py:305
  33.4 3.9 %copy-start.6 = (f32[64,1536]{1,0:T(8,128)S(1)}, f32[64,1536]{1,0:T(8,128)}, u32[]{:S(2)}) copy-start(f32[64,1536]{1,0:T(8,128)} %get-tuple-element.10.basis_ref) | copy-start | bytes 1179652
  33.4 3.9 %copy-start.7 = (f32[3,64,128]{2,1,0:T(8,128)S(1)}, f32[3,64,128]{2,1,0:T(8,128)}, u32[]{:S(2)}) copy-start(f32[3,64,128]{2,1,0:T(8,128)} %get-tuple-element.12.transfer_ref) | copy-start | bytes 294916
  37.3 20.6 %copy-start.2 = (s32[6,8]{1,0:T(8,128)S(1)}, s32[6,8]{1,0:T(8,128)}, u32[]{:S(2)}) copy-start(s32[6,8]{1,0:T(8,128)} %far_ref.2) | copy-start | bytes 580
  37.3 20.6 %copy-start.4 = (s32[6]{0:T(128)S(1)}, s32[6]{0:T(128)}, u32[]{:S(2)}) copy-start(s32[6]{0:T(128)} %count_ref.2) | copy-start | bytes 76
  38.5 14.3 %collective-permute-start.3 = (bf16[192,256]{1,0:T(8,128)(2,1)S(1)}, bf16[192,256]{1,0:T(8,128)(2,1)S(1)}, u32[]{:S(2)}, u32[]{:S(2)}) collective-permute-start(bf16[192,256]{1,0:T(8,128)(2,1)S(1)} %get-tuple-element.23), channel_id=1, source_target_pairs={{0,8},{8,0},{16,24},{24,16},{32,40},{40,32},{48,56},{56,48},{64,72... | collective-permute-start | bytes 294920 | tf_op jit(solution)/shard_map/ppermute | solution.py:348
  41.3 11.4 %collective-permute-start.2 = (bf16[192,256]{1,0:T(8,128)(2,1)S(1)}, bf16[192,256]{1,0:T(8,128)(2,1)S(1)}, u32[]{:S(2)}, u32[]{:S(2)}) collective-permute-start(bf16[192,256]{1,0:T(8,128)(2,1)S(1)} %get-tuple-element.23), channel_id=1, source_target_pairs={{8,16},{16,8},{24,32},{32,24},{40,48},{48,40},{56,64},{64,56},{72,... | collective-permute-start | bytes 294920 | tf_op jit(solution)/shard_map/ppermute | solution.py:348
  47.2 8.9 %collective-permute-start.1 = (bf16[384,256]{1,0:T(8,128)(2,1)S(1)}, bf16[384,256]{1,0:T(8,128)(2,1)S(1)}, u32[]{:S(2)}, u32[]{:S(2)}) collective-permute-start(bf16[384,256]{1,0:T(8,128)(2,1)S(1)} %get-tuple-element.21.refs_0_), channel_id=1, source_target_pairs={{0,1},{1,0},{2,3},{3,2},{4,5},{5,4},{6,7},{7,6},{8,9},{9,8},{10,11... | collective-permute-start | bytes 589832 | tf_op jit(solution)/shard_map/ppermute | solution.py:352
  50.6 7.3 %collective-permute-start = (bf16[384,256]{1,0:T(8,128)(2,1)S(1)}, bf16[384,256]{1,0:T(8,128)(2,1)S(1)}, u32[]{:S(2)}, u32[]{:S(2)}) collective-permute-start(bf16[384,256]{1,0:T(8,128)(2,1)S(1)} %get-tuple-element.21.refs_0_), channel_id=1, source_target_pairs={{1,2},{2,1},{3,4},{4,3},{5,6},{6,5},{7,8},{8,7},{9,10},{10,9},{11,... | collective-permute-start | bytes 589832 | tf_op jit(solution)/shard_map/ppermute | solution.py:352
  52.8 10.9 %collective-permute-start.5 = (bf16[576,256]{1,0:T(8,128)(2,1)S(1)}, bf16[576,256]{1,0:T(8,128)(2,1)S(1)}, u32[]{:S(2)}, u32[]{:S(2)}) collective-permute-start(bf16[576,256]{1,0:T(8,128)(2,1)S(1)} %constant_dynamic-update-slice_fusion.refs_0_), channel_id=1, source_target_pairs={{0,24},{24,0},{48,72},{72,48},{96,120},{120,96},{144,168},{168,144... | collective-permute-start | bytes 884744 | tf_op jit(solution)/shard_map/ppermute | solution.py:354
  54.7 17.6 %collective-permute-start.4 = (bf16[576,256]{1,0:T(8,128)(2,1)S(1)}, bf16[576,256]{1,0:T(8,128)(2,1)S(1)}, u32[]{:S(2)}, u32[]{:S(2)}) collective-permute-start(bf16[576,256]{1,0:T(8,128)(2,1)S(1)} %constant_dynamic-update-slice_fusion.refs_0_), channel_id=1, source_target_pairs={{24,48},{48,24},{72,96},{96,72},{120,144},{144,120},{168,192},{192... | collective-permute-start | bytes 884744 | tf_op jit(solution)/shard_map/ppermute | solution.py:354
  57.9 14.5 %copy-start.3 = (s32[3,8]{1,0:T(4,128)S(1)}, s32[3,8]{1,0:T(4,128)}, u32[]{:S(2)}) copy-start(s32[3,8]{1,0:T(4,128)} %far_ref.3) | copy-start | bytes 292
  57.9 14.5 %copy-start.5 = (s32[3]{0:T(128)S(1)}, s32[3]{0:T(128)}, u32[]{:S(2)}) copy-start(s32[3]{0:T(128)} %count_ref.3) | copy-start | bytes 40

commit v5 on v4

--- a/solution.py
+++ b/solution.py
@@ -318,20 +318,19 @@
 
 
 def far_pairs(rows):
-    sets = [[], []]
-    for start in range(3):
-        for late in range(2):
-            sets[late ^ (start != 1)] += swaps(range(start, rows, 3), late)
-    sets[0] += [(0, 2), (rows - 1, rows - 3)]
+    sets = [sum((swaps(range(start, rows, 3), late) for start in range(3)), []) for late in (1, 0)]
+    edge = [(0, 2), (rows - 1, rows - 3)]
     got = [{r} for r in range(rows)]
     for pairs in sets:
         assert len({i for i, _ in pairs}) == len({j for _, j in pairs}) == len(pairs)
         for i, j in pairs:
             got[j] |= {i - 1, i, i + 1}
+    for i, j in edge:
+        got[j] |= {i}
     for r in range(rows):
         have = got[r] | {r - 1, r + 1}
         assert all(q in have for q in range(max(r - REACH, 0), min(r + REACH + 1, rows)))
-    return sets
+    return *sets, edge
 
 
 def body(sketch, probes, test_leaf, test_parent, leaf_far, leaf_count, parent_far, parent_count):
@@ -352,6 +351,7 @@
     halo = [v] + [lax.ppermute(v, both, pairs[e]) for e in range(2)]
     pairs = far_pairs(row_count)
     far = [lax.ppermute(near, "rows", pairs[e]) for e in range(2)]
+    edge = lax.ppermute(b, "rows", pairs[2])
 
     def leaf_place():
         own = lax.axis_index(both)
@@ -368,11 +368,10 @@
 
     def parent_place():
         row = lax.axis_index("rows")
-        behind = (lax.rem(lax.div(row, 3), 2) == 0) != (lax.rem(row, 3) == 1)
+        behind = lax.rem(lax.div(row, 3), 2) == 0
         one = jnp.where(behind, -(REACH - 1), REACH - 1)
         two = -one
-        one = jnp.where(row == 2, -2, one)
-        one = jnp.where(row == row_count - 3, 2, one)
+        last = row_count - 1
         across = per_device * samp_count
 
         def spot(parent):
@@ -384,12 +383,14 @@
 
             far_at = jnp.where(abs(away - one) <= 1, 3 + among(away - one, one), 6 + among(away - two, two))
             at = jnp.where(abs(away) <= 1, among(away, 0), far_at)
+            beyond = ((row == 2) & (away == -2)) | ((row == last - 2) & (away == 2))
+            at = jnp.where(beyond, 9, at)
             return at * per_device + lax.rem(parent, per_device)
 
         return spot
 
     leaf_coupling = run_couple(leaf_place, leaf_far, leaf_count, w, halo)
-    parent_coupling = run_couple(parent_place, parent_far, parent_count, a, [near, *far])
+    parent_coupling = run_couple(parent_place, parent_far, parent_count, a, [near, *far, edge])
     return (basis, leaf_coupling, transfer, parent_coupling)
 
 

time: 74.8 us -> 72.1 us (0.964)
  the two profiles are of different devices: /device:TPU:5 before, /device:TPU:4 now
where the time goes in v5:
time: 72.1 us; the launch traced here: 71.7 us
  starting transfers between devices  25.8 us (36%)
  waiting for transfers between devices  25.8 us (36%)
  Pallas kernels  16.7 us (23%)
  other arithmetic  2.43 us (3%)
  between operations  0.91 us (1%)
    all_to_all x2, waiting for transfers between devices, gathered(): got = lax.all_to_all(sent, 'samp', split_axis=0, concat_axis=0, tiled=True)  15 us
    ppermute x2, waiting for transfers between devices, body(): halo = [v] + [lax.ppermute(v, both, pairs[e]) for e in range(2)]  10.8 us
    ppermute x2, starting transfers between devices, body(): near = [b] + [lax.ppermute(b, 'rows', pairs[e]) for e in range(2)]  9.24 us
    pallas_call x1, Pallas kernels, run_compress(): pl.pallas_call(compress, out_shape=(jax.ShapeDtypeStruct((RANK, y.shape[1...  8.32 us
    all_to_all x2, starting transfers between devices, gathered(): got = lax.all_to_all(sent, 'samp', split_axis=0, concat_axis=0, tiled=True)  8.02 us
    ppermute x2, starting transfers between devices, body(): halo = [v] + [lax.ppermute(v, both, pairs[e]) for e in range(2)]  4.54 us
    pallas_call x2, Pallas kernels, run_couple(): pl.pallas_call(functools.partial(couple, place), out_shape=jax.ShapeDtype...  4.14 us
    pallas_call x2, Pallas kernels, run_pack(): pl.pallas_call(pack, out_shape=jax.ShapeDtypeStruct((parts, rows, columns...  3.08 us
  transfers between devices with their start and end apart: 9, of which 3 were waited for; matrix products, arithmetic and copies ran while one was open for 2% of the time, Pallas kernels for 17%

profile of v5, /device:TPU:4, one launch (start us, length us, event | category | flops | bytes accessed | tf_op | source)
XLA Modules:
  0.0 71.7 jit_solution(6243202207538746507)
XLA Ops:
  0.6 1.5 %pack.2 = f32[8,32,1536]{2,1,0:T(8,128)S(1)} custom-call(f32[32,12288]{1,0:T(8,128)} %x_ref.2), custom_call_target="tpu_custom_call" | custom-call | flops 1000000000 | bytes 1000000 | tf_op jit(solution)/shard_map/pack/pallas_call | solution.py:220
  2.2 1.0 %multiply_convert_fusion.1 = f16[8,32,1536]{2,1,0:T(8,128)(2,1)} fusion(f32[8,32,1536]{2,1,0:T(8,128)S(1)} %pack.2), kind=kLoop, calls=%fused_computation.3 | loop fusion | flops 786432 | bytes 2359296 | tf_op jit(solution)/shard_map/convert_element_type | solution.py:304
  3.2 4.5 %all-to-all-start = ((f16[8,32,1536]{2,1,0:T(8,128)(2,1)}), f16[8,32,1536]{2,1,0:T(8,128)(2,1)S(1)}, u32[]{:S(2)}, u32[]{:S(2)}) async-start(f16[8,32,1536]{2,1,0:T(8,128)(2,1)} %multiply_convert_fusion.1), calls=%async_computation | async-start | bytes 1572864 | tf_op jit(solution)/shard_map/all_to_all | solution.py:305
  7.6 0.0 copy-start
  7.7 0.0 copy-start.1
  7.7 1.6 %pack.3 = f32[8,32,1536]{2,1,0:T(8,128)S(1)} custom-call(f32[32,12288]{1,0:T(8,128)} %x_ref.3), custom_call_target="tpu_custom_call" | custom-call | flops 1000000000 | bytes 1000000 | tf_op jit(solution)/shard_map/pack/pallas_call | solution.py:220
  9.2 0.0 copy-done
  9.2 0.0 copy-done.1
  9.3 1.0 %multiply_convert_fusion = f16[8,32,1536]{2,1,0:T(8,128)(2,1)} fusion(f32[8,32,1536]{2,1,0:T(8,128)S(1)} %pack.3), kind=kLoop, calls=%fused_computation.1 | loop fusion | flops 786432 | bytes 2359296 | tf_op jit(solution)/shard_map/convert_element_type | solution.py:304
  10.3 10.5 %all-to-all-done = f16[8,32,1536]{2,1,0:T(8,128)(2,1)S(1)} async-done(((f16[8,32,1536]{2,1,0:T(8,128)(2,1)}), f16[8,32,1536]{2,1,0:T(8,128)(2,1)S(1)}, u32[]{:S(2)}, u32[]{:S(2)}) %all-to-all-start) | async-done | bytes 786464 | tf_op jit(solution)/shard_map/all_to_all | solution.py:305
  20.8 3.5 %all-to-all-start.1 = ((f16[8,32,1536]{2,1,0:T(8,128)(2,1)}), f16[8,32,1536]{2,1,0:T(8,128)(2,1)S(1)}, u32[]{:S(2)}, u32[]{:S(2)}) async-start(f16[8,32,1536]{2,1,0:T(8,128)(2,1)} %multiply_convert_fusion), calls=%async_computation.1 | async-start | bytes 1572864 | tf_op jit(solution)/shard_map/all_to_all | solution.py:305
  24.3 0.2 convert_multiply_fusion.1
  24.5 8.3 %compress.1 = (f32[64,1536]{1,0:T(8,128)}, bf16[384,256]{1,0:T(8,128)(2,1)S(1)}, f32[3,64,128]{2,1,0:T(8,128)}, bf16[192,256]{1,0:T(8,128)(2,1)S(1)}) custom-call(f32[256,1536]{1,0:T(8,128)S(1)} %bitcast.12, bf16[64,256]{1,0:T(8,128)(2,1)S(1)} %get-tuple-element.14.test_high, bf16[64,256]{1,0:T(8,128)(2,1)S(1)} %get-tuple-element.15.test_low, ...), custom_call_target="tpu_custom_call" | custom-call | flops 12000000000 | bytes 12000000 | tf_op jit(solution)/shard_map/compress/pallas_call | solution.py:247
  32.9 0.0 copy-start.6
  32.9 0.0 copy-start.7
  32.9 4.5 %all-to-all-done.1 = f16[8,32,1536]{2,1,0:T(8,128)(2,1)S(1)} async-done(((f16[8,32,1536]{2,1,0:T(8,128)(2,1)}), f16[8,32,1536]{2,1,0:T(8,128)(2,1)S(1)}, u32[]{:S(2)}, u32[]{:S(2)}) %all-to-all-start.1) | async-done | bytes 786464 | tf_op jit(solution)/shard_map/all_to_all | solution.py:305
  37.4 0.2 convert_multiply_fusion
  37.6 0.0 copy-done.6
  37.6 0.0 copy-done.7
  37.6 0.0 copy-start.2
  37.6 0.0 copy-start.4
  37.6 1.1 %project.1 = (bf16[384,256]{1,0:T(8,128)(2,1)S(1)}, bf16[192,256]{1,0:T(8,128)(2,1)S(1)}) custom-call(f32[256,1536]{1,0:T(8,128)S(1)} %bitcast.13, f32[64,1536]{1,0:T(8,128)S(1)} %copy-done.6, f32[3,64,128]{2,1,0:T(8,128)S(1)} %copy-done.7), custom_call_target="tpu_custom_call" | custom-call | flops 4000000000 | bytes 4000000 | tf_op jit(solution)/shard_map/project/pallas_call | solution.py:267
  38.7 3.1 %collective-permute-start.3 = (bf16[192,256]{1,0:T(8,128)(2,1)S(1)}, bf16[192,256]{1,0:T(8,128)(2,1)S(1)}, u32[]{:S(2)}, u32[]{:S(2)}) collective-permute-start(bf16[192,256]{1,0:T(8,128)(2,1)S(1)} %get-tuple-element.23), channel_id=1, source_target_pairs={{0,8},{8,0},{16,24},{24,16},{32,40},{40,32},{48,56},{56,48},{64,72... | collective-permute-start | bytes 294920 | tf_op jit(solution)/shard_map/ppermute | solution.py:347
  41.9 6.1 %collective-permute-start.2 = (bf16[192,256]{1,0:T(8,128)(2,1)S(1)}, bf16[192,256]{1,0:T(8,128)(2,1)S(1)}, u32[]{:S(2)}, u32[]{:S(2)}) collective-permute-start(bf16[192,256]{1,0:T(8,128)(2,1)S(1)} %get-tuple-element.23), channel_id=1, source_target_pairs={{8,16},{16,8},{24,32},{32,24},{40,48},{48,40},{56,64},{64,56},{72,... | collective-permute-start | bytes 294920 | tf_op jit(solution)/shard_map/ppermute | solution.py:347
  48.0 1.9 %collective-permute-start.1 = (bf16[384,256]{1,0:T(8,128)(2,1)S(1)}, bf16[384,256]{1,0:T(8,128)(2,1)S(1)}, u32[]{:S(2)}, u32[]{:S(2)}) collective-permute-start(bf16[384,256]{1,0:T(8,128)(2,1)S(1)} %get-tuple-element.21.refs_0_), channel_id=1, source_target_pairs={{0,1},{1,0},{2,3},{3,2},{4,5},{5,4},{6,7},{7,6},{8,9},{9,8},{10,11... | collective-permute-start | bytes 589832 | tf_op jit(solution)/shard_map/ppermute | solution.py:351
  49.9 2.6 %collective-permute-start = (bf16[384,256]{1,0:T(8,128)(2,1)S(1)}, bf16[384,256]{1,0:T(8,128)(2,1)S(1)}, u32[]{:S(2)}, u32[]{:S(2)}) collective-permute-start(bf16[384,256]{1,0:T(8,128)(2,1)S(1)} %get-tuple-element.21.refs_0_), channel_id=1, source_target_pairs={{1,2},{2,1},{3,4},{4,3},{5,6},{6,5},{7,8},{8,7},{9,10},{10,9},{11,... | collective-permute-start | bytes 589832 | tf_op jit(solution)/shard_map/ppermute | solution.py:351
  52.6 0.0 collective-permute-done.2
  52.6 0.0 collective-permute-done.3
  52.6 2.0 %collective-permute-start.5 = (bf16[576,256]{1,0:T(8,128)(2,1)S(1)}, bf16[576,256]{1,0:T(8,128)(2,1)S(1)}, u32[]{:S(2)}, u32[]{:S(2)}) collective-permute-start(bf16[576,256]{1,0:T(8,128)(2,1)S(1)} %constant_dynamic-update-slice_fusion.refs_0_), channel_id=1, source_target_pairs={{0,24},{24,0},{48,72},{72,48},{96,120},{120,96},{144,168},{168,144... | collective-permute-start | bytes 884744 | tf_op jit(solution)/shard_map/ppermute | solution.py:353
  54.7 0.7 collective-permute-start.4
  55.3 1.3 %collective-permute-start.6 = (bf16[192,256]{1,0:T(8,128)(2,1)S(1)}, bf16[192,256]{1,0:T(8,128)(2,1)S(1)}, u32[]{:S(2)}, u32[]{:S(2)}) collective-permute-start(bf16[192,256]{1,0:T(8,128)(2,1)S(1)} %get-tuple-element.23), channel_id=1, source_target_pairs={{0,16},{504,488},{1,17},{505,489},{2,18},{506,490},{3,19},{507,491... | collective-permute-start | bytes 294920 | tf_op jit(solution)/shard_map/ppermute | solution.py:354
  56.6 0.0 collective-permute-done.1.refs_2_
  56.7 10.8 %collective-permute-done.refs_1_ = bf16[384,256]{1,0:T(8,128)(2,1)S(1)} collective-permute-done((bf16[384,256]{1,0:T(8,128)(2,1)S(1)}, bf16[384,256]{1,0:T(8,128)(2,1)S(1)}, u32[]{:S(2)}, u32[]{:S(2)}) %collective-permute-start) | collective-permute-done | bytes 196640 | tf_op jit(solution)/shard_map/ppermute | solution.py:351
  67.5 0.0 copy-done.2
  67.5 0.0 copy-done.4
  67.5 0.0 copy-start.3
  67.5 0.0 copy-start.5
  67.5 2.1 %shard_map.111 = f32[1536,128]{1,0:T(8,128)} custom-call(s32[6,8]{1,0:T(8,128)S(1)} %copy-done.2, s32[6]{0:T(128)S(1)} %copy-done.4, bf16[384,256]{1,0:T(8,128)(2,1)S(1)} %get-tuple-element.19.left_ref, bf16[384,256]{1,0:T(8,128)(2,1)S(1)} %get-tuple-element.21.refs_0_, bf16[384,256]{1,0:T(8,128)(2,1)S(1)} %collective-permute-done.refs_1_, ...), custom_call_target="tpu_custom_call" | custom-call | flops 3000000000 | bytes 3000000 | tf_op jit(solution)/shard_map/pallas_call | solution.py:284
  69.6 0.0 collective-permute-done.6.refs_3_
  69.6 0.0 collective-permute-done.5.refs_2_
  69.6 0.0 collective-permute-done.4.refs_1_
  69.6 0.0 copy-done.3
  69.6 0.0 copy-done.5
  69.6 2.1 %shard_map.112 = f32[768,128]{1,0:T(8,128)} custom-call(s32[3,8]{1,0:T(4,128)S(1)} %copy-done.3, s32[3]{0:T(128)S(1)} %copy-done.5, bf16[192,256]{1,0:T(8,128)(2,1)S(1)} %get-tuple-element.22.left_ref, bf16[576,256]{1,0:T(8,128)(2,1)S(1)} %constant_dynamic-update-slice_fusion.refs_0_, bf16[576,256]{1,0:T(8,128)(2,1)S(1)} %collective-permute-done.4.refs_1_, ...), custom_call_target="tpu_custom_call" | custom-call | flops 3000000000 | bytes 3000000 | tf_op jit(solution)/shard_map/pallas_call | solution.py:284
  (4 shorter events, 0.0 us)
Async XLA Ops:
  3.2 17.6 %all-to-all-start = ((f16[8,32,1536]{2,1,0:T(8,128)(2,1)}), f16[8,32,1536]{2,1,0:T(8,128)(2,1)S(1)}, u32[]{:S(2)}, u32[]{:S(2)}) async-start(f16[8,32,1536]{2,1,0:T(8,128)(2,1)} %multiply_convert_fusion.1), calls=%async_computation | async-start | bytes 1572864 | tf_op jit(solution)/shard_map/all_to_all | solution.py:305
  7.6 1.6 %copy-start = (f32[64,256]{1,0:T(8,128)S(1)}, f32[64,256]{1,0:T(8,128)}, u32[]{:S(2)}) copy-start(f32[64,256]{1,0:T(8,128)} %refs_0_.1) | copy-start | bytes 196612
  7.7 1.6 %copy-start.1 = (f32[64,256]{1,0:T(8,128)S(1)}, f32[64,256]{1,0:T(8,128)}, u32[]{:S(2)}) copy-start(f32[64,256]{1,0:T(8,128)} %refs_1_.1) | copy-start | bytes 196612
  20.8 16.6 %all-to-all-start.1 = ((f16[8,32,1536]{2,1,0:T(8,128)(2,1)}), f16[8,32,1536]{2,1,0:T(8,128)(2,1)S(1)}, u32[]{:S(2)}, u32[]{:S(2)}) async-start(f16[8,32,1536]{2,1,0:T(8,128)(2,1)} %multiply_convert_fusion), calls=%async_computation.1 | async-start | bytes 1572864 | tf_op jit(solution)/shard_map/all_to_all | solution.py:305
  32.9 4.7 %copy-start.6 = (f32[64,1536]{1,0:T(8,128)S(1)}, f32[64,1536]{1,0:T(8,128)}, u32[]{:S(2)}) copy-start(f32[64,1536]{1,0:T(8,128)} %get-tuple-element.10.basis_ref) | copy-start | bytes 1179652
  32.9 4.7 %copy-start.7 = (f32[3,64,128]{2,1,0:T(8,128)S(1)}, f32[3,64,128]{2,1,0:T(8,128)}, u32[]{:S(2)}) copy-start(f32[3,64,128]{2,1,0:T(8,128)} %get-tuple-element.12.transfer_ref) | copy-start | bytes 294916
  37.6 29.9 %copy-start.2 = (s32[6,8]{1,0:T(8,128)S(1)}, s32[6,8]{1,0:T(8,128)}, u32[]{:S(2)}) copy-start(s32[6,8]{1,0:T(8,128)} %far_ref.2) | copy-start | bytes 580
  37.6 29.8 %copy-start.4 = (s32[6]{0:T(128)S(1)}, s32[6]{0:T(128)}, u32[]{:S(2)}) copy-start(s32[6]{0:T(128)} %count_ref.2) | copy-start | bytes 76
  38.7 13.9 %collective-permute-start.3 = (bf16[192,256]{1,0:T(8,128)(2,1)S(1)}, bf16[192,256]{1,0:T(8,128)(2,1)S(1)}, u32[]{:S(2)}, u32[]{:S(2)}) collective-permute-start(bf16[192,256]{1,0:T(8,128)(2,1)S(1)} %get-tuple-element.23), channel_id=1, source_target_pairs={{0,8},{8,0},{16,24},{24,16},{32,40},{40,32},{48,56},{56,48},{64,72... | collective-permute-start | bytes 294920 | tf_op jit(solution)/shard_map/ppermute | solution.py:347
  41.9 10.7 %collective-permute-start.2 = (bf16[192,256]{1,0:T(8,128)(2,1)S(1)}, bf16[192,256]{1,0:T(8,128)(2,1)S(1)}, u32[]{:S(2)}, u32[]{:S(2)}) collective-permute-start(bf16[192,256]{1,0:T(8,128)(2,1)S(1)} %get-tuple-element.23), channel_id=1, source_target_pairs={{8,16},{16,8},{24,32},{32,24},{40,48},{48,40},{56,64},{64,56},{72,... | collective-permute-start | bytes 294920 | tf_op jit(solution)/shard_map/ppermute | solution.py:347
  48.0 8.6 %collective-permute-start.1 = (bf16[384,256]{1,0:T(8,128)(2,1)S(1)}, bf16[384,256]{1,0:T(8,128)(2,1)S(1)}, u32[]{:S(2)}, u32[]{:S(2)}) collective-permute-start(bf16[384,256]{1,0:T(8,128)(2,1)S(1)} %get-tuple-element.21.refs_0_), channel_id=1, source_target_pairs={{0,1},{1,0},{2,3},{3,2},{4,5},{5,4},{6,7},{7,6},{8,9},{9,8},{10,11... | collective-permute-start | bytes 589832 | tf_op jit(solution)/shard_map/ppermute | solution.py:351
  49.9 17.5 %collective-permute-start = (bf16[384,256]{1,0:T(8,128)(2,1)S(1)}, bf16[384,256]{1,0:T(8,128)(2,1)S(1)}, u32[]{:S(2)}, u32[]{:S(2)}) collective-permute-start(bf16[384,256]{1,0:T(8,128)(2,1)S(1)} %get-tuple-element.21.refs_0_), channel_id=1, source_target_pairs={{1,2},{2,1},{3,4},{4,3},{5,6},{6,5},{7,8},{8,7},{9,10},{10,9},{11,... | collective-permute-start | bytes 589832 | tf_op jit(solution)/shard_map/ppermute | solution.py:351
  52.6 17.0 %collective-permute-start.5 = (bf16[576,256]{1,0:T(8,128)(2,1)S(1)}, bf16[576,256]{1,0:T(8,128)(2,1)S(1)}, u32[]{:S(2)}, u32[]{:S(2)}) collective-permute-start(bf16[576,256]{1,0:T(8,128)(2,1)S(1)} %constant_dynamic-update-slice_fusion.refs_0_), channel_id=1, source_target_pairs={{0,24},{24,0},{48,72},{72,48},{96,120},{120,96},{144,168},{168,144... | collective-permute-start | bytes 884744 | tf_op jit(solution)/shard_map/ppermute | solution.py:353
  54.7 14.9 %collective-permute-start.4 = (bf16[576,256]{1,0:T(8,128)(2,1)S(1)}, bf16[576,256]{1,0:T(8,128)(2,1)S(1)}, u32[]{:S(2)}, u32[]{:S(2)}) collective-permute-start(bf16[576,256]{1,0:T(8,128)(2,1)S(1)} %constant_dynamic-update-slice_fusion.refs_0_), channel_id=1, source_target_pairs={{24,48},{48,24},{72,96},{96,72},{120,144},{144,120},{168,192},{192... | collective-permute-start | bytes 884744 | tf_op jit(solution)/shard_map/ppermute | solution.py:353
  55.3 14.2 %collective-permute-start.6 = (bf16[192,256]{1,0:T(8,128)(2,1)S(1)}, bf16[192,256]{1,0:T(8,128)(2,1)S(1)}, u32[]{:S(2)}, u32[]{:S(2)}) collective-permute-start(bf16[192,256]{1,0:T(8,128)(2,1)S(1)} %get-tuple-element.23), channel_id=1, source_target_pairs={{0,16},{504,488},{1,17},{505,489},{2,18},{506,490},{3,19},{507,491... | collective-permute-start | bytes 294920 | tf_op jit(solution)/shard_map/ppermute | solution.py:354
  67.5 2.1 %copy-start.3 = (s32[3,8]{1,0:T(4,128)S(1)}, s32[3,8]{1,0:T(4,128)}, u32[]{:S(2)}) copy-start(s32[3,8]{1,0:T(4,128)} %far_ref.3) | copy-start | bytes 292
  67.5 2.1 %copy-start.5 = (s32[3]{0:T(128)S(1)}, s32[3]{0:T(128)}, u32[]{:S(2)}) copy-start(s32[3]{0:T(128)} %count_ref.3) | copy-start | bytes 40
